TPU v7x, 512 devices: a whole 4x8x8 slice. The times are simulated.
512 devices in a mesh: src: 4 (over y_hi), rcv: 16 (over z, y_lo), freq: 8 (over x, core).
Axes of the slice: x: 4, y: 8 (y_hi: 4, y_lo: 2; y = y_hi * 2 + y_lo), z: 8, core: 2. Of those that a mesh axis runs over, the one named last changes fastest.
Arguments:
- wavefield: float32 [2, 8, 2048, 2048], P(None, 'freq', 'src', 'rcv'), may hold values from -6 to 6
- op_table: float32 [2, 64, 19], replicated, may hold values from -1.2 to 1.2
- vel_index: int32 [128], replicated, may hold values from 0 to 15
- interp_index: int32 [16, 8], replicated, may hold values from 0 to 62
- interp_weight: float32 [16, 8], replicated, may hold values from 0 to 1
- freq_perm: int32 [8], P('freq'), may hold values from 0 to 7, each once
Outputs:
- sunk: float32 [2, 8, 2048, 2048], P(None, 'freq', 'src', 'rcv')
- image: float32 [2048], P('rcv')
Inputs may be any that keep to these rules, and one draw needn't show every extreme that they name: `freq_perm`: each of the 8 frequencies is held by exactly one slot.
All inputs are finite; a program needn't handle non-finite values.
Results may differ from a plain program's by a relative error of at most 0.00012.
Values sent between devices are 32-bit elements; how exact they have to be, the bound alone decides.
A program may use at most 64 MiB of HBM per device.

v0:
```python
import jax
import jax.numpy as jnp
from jax import lax
from jax.sharding import PartitionSpec as P

SUBSTEPS = 4
TILE = 16


def extended(shard, sides, width):
    for axis, dim in sides:
        size, length = (lax.axis_size(axis), shard.shape[dim])
        up = [(i, (i + 1) % size) for i in range(size - 1)]
        down = [(j, i) for i, j in up]
        last = lax.slice_in_dim(shard, length - width, length, axis=dim)
        first = lax.slice_in_dim(shard, 0, width, axis=dim)
        before = lax.ppermute(last, axis, up)
        after = lax.ppermute(first, axis, down)
        shard = jnp.concatenate([before, shard, after], axis=dim)
    return shard


def from_everyone(shard, axis):
    size = lax.axis_size(axis)
    return lax.all_to_all(
        jnp.broadcast_to(shard[None], (size, *shard.shape)), axis, 0, 0, tiled=True
    )


def of_everyone(shard, axis):
    everything = from_everyone(shard, axis)
    return jnp.sum(everything, axis=0)


def convolve(padded, coefficients, along_axis, span_width):
    out_shape = list(padded.shape[1:])
    out_shape[along_axis - 1] = span_width
    zeros_init = jnp.zeros(tuple(out_shape), jnp.float32)

    def add_tap(tap_index, totals):
        window = lax.dynamic_slice_in_dim(padded, tap_index, span_width, axis=along_axis)
        coef_tap = lax.dynamic_index_in_dim(coefficients, tap_index, axis=2, keepdims=False)
        coef_real = coef_tap[0]
        coef_imag = coef_tap[1]
        if along_axis == 3:
            coef_real = coef_real[:, None, :]
            coef_imag = coef_imag[:, None, :]
        else:
            coef_real = coef_real[:, :, None]
            coef_imag = coef_imag[:, :, None]
        real_sum = totals[0] + (coef_real * window[0] - coef_imag * window[1])
        imag_sum = totals[1] + (coef_real * window[1] + coef_imag * window[0])
        return (real_sum, imag_sum)

    real_acc, imag_acc = lax.fori_loop(0, coefficients.shape[2], add_tap, (zeros_init, zeros_init))
    return jnp.stack([real_acc, imag_acc])


def build_taps(op_table, interp_index, interp_weight, freq_ids):
    freq_count = interp_index.shape[1]
    table_len = op_table.shape[1]
    pick_freq = freq_ids[:, None] == jnp.arange(freq_count, dtype=jnp.int32)[None, :]
    table_row = jnp.sum(jnp.where(pick_freq[None], interp_index[:, None, :], 0), axis=2)
    weights = jnp.sum(jnp.where(pick_freq[None], interp_weight[:, None, :], 0.0), axis=2)
    rows_iota = jnp.arange(table_len, dtype=jnp.int32)
    pick_lower = table_row[:, :, None] == rows_iota
    pick_upper = (table_row + 1)[:, :, None] == rows_iota
    lower_taps = jnp.sum(
        jnp.where(pick_lower[None, :, :, :, None], op_table[:, None, None, :, :], 0.0), axis=3
    )
    upper_taps = jnp.sum(
        jnp.where(pick_upper[None, :, :, :, None], op_table[:, None, None, :, :], 0.0), axis=3
    )
    mixed = lower_taps * (1.0 - weights)[None, :, :, None] + upper_taps * weights[None, :, :, None]
    return jnp.transpose(mixed, (0, 2, 3, 1))


def coefficients_at(mixed_taps, vel_index, positions, lateral):
    tile_count = vel_index.shape[0]
    vel_count = mixed_taps.shape[3]
    tile_of = jnp.clip(positions, 0, lateral - 1) // TILE
    pick_tile = tile_of[:, None] == jnp.arange(tile_count, dtype=jnp.int32)[None, :]
    velocity = jnp.sum(jnp.where(pick_tile, vel_index[None, :], 0), axis=1)
    pick_velocity = (velocity[:, None] == jnp.arange(vel_count, dtype=jnp.int32)[None, :]).astype(
        jnp.float32
    )
    return jnp.einsum("cfkv,xv->cfkx", mixed_taps, pick_velocity, precision=lax.Precision.HIGHEST)


def body(wavefield, op_table, vel_index, interp_index, interp_weight, freq_perm):
    src_rows = wavefield.shape[2]
    rcv_cols = wavefield.shape[3]
    lateral = rcv_cols * lax.axis_size("rcv")
    half_taps = op_table.shape[2] // 2
    mixed_taps = build_taps(op_table, interp_index, interp_weight, freq_perm)
    col_start = lax.axis_index("rcv") * rcv_cols
    row_start = lax.axis_index("src") * src_rows
    wave_field = wavefield
    col_positions = col_start + jnp.arange(rcv_cols, dtype=jnp.int32)
    rcv_coefficients = coefficients_at(mixed_taps, vel_index, col_positions, lateral)
    for substep in range(SUBSTEPS):
        padded = extended(wave_field, (("rcv", 3),), half_taps)
        wave_field = convolve(padded, rcv_coefficients, 3, rcv_cols)
    row_positions = row_start + jnp.arange(src_rows, dtype=jnp.int32)
    src_coefficients = coefficients_at(mixed_taps, vel_index, row_positions, lateral)
    for substep in range(SUBSTEPS):
        padded = extended(wave_field, (("src", 2),), half_taps)
        wave_field = convolve(padded, src_coefficients, 2, src_rows)
    offset = col_start - row_start
    valid = (offset >= 0) & (offset < src_rows)
    start = jnp.clip(offset, 0, src_rows - rcv_cols)
    diag_block = lax.dynamic_slice_in_dim(wave_field[0], start, rcv_cols, axis=1)
    diagonal_sum = jnp.sum(jnp.diagonal(diag_block, axis1=1, axis2=2), axis=0)
    local_image = jnp.where(valid, diagonal_sum, 0.0)
    zero_image = of_everyone(local_image, ("src", "freq"))
    return (wave_field, zero_image)


def solution(mesh):
    in_specs = (P(None, "freq", "src", "rcv"), P(), P(), P(), P(), P("freq"))
    out_specs = (P(None, "freq", "src", "rcv"), P("rcv"))
    return jax.shard_map(body, mesh=mesh, in_specs=in_specs, out_specs=out_specs, check_vma=False)
```

profile of v0, /device:TPU:1, one launch (start us, length us, event | category | flops | bytes accessed | tf_op | source)
XLA Modules:
  0.0 230.6 jit_solution(13475911836250076661)
XLA Ops:
  0.6 1.5 fusion.22
  2.2 4.1 %collective-permute-start = (f32[2,1,512,9]{3,2,1,0:T(8,128)S(1)}, f32[2,1,512,9]{3,2,1,0:T(8,128)S(1)}, u32[]{:S(2)}, u32[]{:S(2)}) collective-permute-start(f32[2,1,512,9]{3,2,1,0:T(8,128)S(1)} %get-tuple-element.1210), channel_id=1, source_target_pairs={{0,8},{8,16},{16,24},{24,32},{32,40},{40,48},{48,56},{56,64},{64,7... | collective-permute-start | bytes 110600 | tf_op jit(solution)/shard_map/ppermute | solution.py:17
  6.3 1.3 collective-permute-start.1
  10.4 3.2 %collective-permute-done = f32[2,1,512,9]{3,2,1,0:T(8,128)S(1)} collective-permute-done((f32[2,1,512,9]{3,2,1,0:T(8,128)S(1)}, f32[2,1,512,9]{3,2,1,0:T(8,128)S(1)}, u32[]{:S(2)}, u32[]{:S(2)}) %collective-permute-start) | collective-permute-done | bytes 36896 | tf_op jit(solution)/shard_map/ppermute | solution.py:17
  13.7 17.1 %collective-permute-done.1 = f32[2,1,512,9]{3,2,1,0:T(8,128)S(1)} collective-permute-done((f32[2,1,512,9]{3,2,1,0:T(8,128)S(1)}, f32[2,1,512,9]{3,2,1,0:T(8,128)S(1)}, u32[]{:S(2)}, u32[]{:S(2)}) %collective-permute-start.1) | collective-permute-done | bytes 36896 | tf_op jit(solution)/shard_map/ppermute | solution.py:18
  31.3 6.6 %while.128 = (s32[]{:T(128)}, f32[1,512,128]{2,1,0:T(8,128)S(1)}, f32[1,512,128]{2,1,0:T(8,128)S(1)}, f32[2,1,19,128]{3,2,1,0:T(8,128)S(1)}, f32[2,1,512,146]{3,2,1,0:T(8,128)S(1)}, /*index=5*/s32[]{:T(128)}, s32[]{:T(128)}, s32[]{}) while((s32[]{:T(128)}, f32[1,512,128]{2,1,0:T(8,128)S(1)}, f32[1,512,128]{2,1,0:T(8,128)S(1)}, ...), condition=%wide.region_6.7_spmd.clone, body=%wide.region_5.6_spmd.clone.sunk | while | flops 655364 | bytes 1576059 | solution.py:55
  38.0 3.2 %collective-permute-start.2 = (f32[2,1,512,9]{3,2,1,0:T(8,128)S(1)}, f32[2,1,512,9]{3,2,1,0:T(8,128)S(1)}, u32[]{:S(2)}, u32[]{:S(2)}) collective-permute-start(f32[2,1,512,9]{3,2,1,0:T(8,128)S(1)} %get-tuple-element.1208), channel_id=1, source_target_pairs={{0,8},{8,16},{16,24},{24,32},{32,40},{40,48},{48,56},{56,64},{64,7... | collective-permute-start | bytes 110600 | tf_op jit(solution)/shard_map/ppermute | solution.py:17
  42.6 8.4 %collective-permute-done.2 = f32[2,1,512,9]{3,2,1,0:T(8,128)S(1)} collective-permute-done((f32[2,1,512,9]{3,2,1,0:T(8,128)S(1)}, f32[2,1,512,9]{3,2,1,0:T(8,128)S(1)}, u32[]{:S(2)}, u32[]{:S(2)}) %collective-permute-start.2) | collective-permute-done | bytes 36896 | tf_op jit(solution)/shard_map/ppermute | solution.py:17
  51.0 13.9 %collective-permute-done.3 = f32[2,1,512,9]{3,2,1,0:T(8,128)S(1)} collective-permute-done((f32[2,1,512,9]{3,2,1,0:T(8,128)S(1)}, f32[2,1,512,9]{3,2,1,0:T(8,128)S(1)}, u32[]{:S(2)}, u32[]{:S(2)}) %collective-permute-start.3) | collective-permute-done | bytes 36896 | tf_op jit(solution)/shard_map/ppermute | solution.py:18
  65.4 6.6 %while.129 = (s32[]{:T(128)}, f32[1,512,128]{2,1,0:T(8,128)S(1)}, f32[1,512,128]{2,1,0:T(8,128)S(1)}, f32[2,1,19,128]{3,2,1,0:T(8,128)S(1)}, f32[2,1,512,146]{3,2,1,0:T(8,128)S(1)}, /*index=5*/s32[]{:T(128)}, s32[]{:T(128)}, s32[]{}) while((s32[]{:T(128)}, f32[1,512,128]{2,1,0:T(8,128)S(1)}, f32[1,512,128]{2,1,0:T(8,128)S(1)}, ...), condition=%wide.region_8.9_spmd.clone, body=%wide.region_7.8_spmd.clone.sunk | while | flops 655364 | bytes 1576059 | solution.py:55
  72.2 3.2 %collective-permute-start.4 = (f32[2,1,512,9]{3,2,1,0:T(8,128)S(1)}, f32[2,1,512,9]{3,2,1,0:T(8,128)S(1)}, u32[]{:S(2)}, u32[]{:S(2)}) collective-permute-start(f32[2,1,512,9]{3,2,1,0:T(8,128)S(1)} %get-tuple-element.1206), channel_id=1, source_target_pairs={{0,8},{8,16},{16,24},{24,32},{32,40},{40,48},{48,56},{56,64},{64,7... | collective-permute-start | bytes 110600 | tf_op jit(solution)/shard_map/ppermute | solution.py:17
  76.8 7.5 %collective-permute-done.4 = f32[2,1,512,9]{3,2,1,0:T(8,128)S(1)} collective-permute-done((f32[2,1,512,9]{3,2,1,0:T(8,128)S(1)}, f32[2,1,512,9]{3,2,1,0:T(8,128)S(1)}, u32[]{:S(2)}, u32[]{:S(2)}) %collective-permute-start.4) | collective-permute-done | bytes 36896 | tf_op jit(solution)/shard_map/ppermute | solution.py:17
  84.3 13.9 %collective-permute-done.5 = f32[2,1,512,9]{3,2,1,0:T(8,128)S(1)} collective-permute-done((f32[2,1,512,9]{3,2,1,0:T(8,128)S(1)}, f32[2,1,512,9]{3,2,1,0:T(8,128)S(1)}, u32[]{:S(2)}, u32[]{:S(2)}) %collective-permute-start.5) | collective-permute-done | bytes 36896 | tf_op jit(solution)/shard_map/ppermute | solution.py:18
  98.7 6.6 %while.130 = (s32[]{:T(128)}, f32[1,512,128]{2,1,0:T(8,128)S(1)}, f32[1,512,128]{2,1,0:T(8,128)S(1)}, f32[2,1,19,128]{3,2,1,0:T(8,128)S(1)}, f32[2,1,512,146]{3,2,1,0:T(8,128)S(1)}, /*index=5*/s32[]{:T(128)}, s32[]{:T(128)}, s32[]{}) while((s32[]{:T(128)}, f32[1,512,128]{2,1,0:T(8,128)S(1)}, f32[1,512,128]{2,1,0:T(8,128)S(1)}, ...), condition=%wide.region_10.11_spmd.clone, body=%wide.region_9.10_spmd.clone.sunk | while | flops 655364 | bytes 1576059 | solution.py:55
  105.5 3.2 %collective-permute-start.6 = (f32[2,1,512,9]{3,2,1,0:T(8,128)S(1)}, f32[2,1,512,9]{3,2,1,0:T(8,128)S(1)}, u32[]{:S(2)}, u32[]{:S(2)}) collective-permute-start(f32[2,1,512,9]{3,2,1,0:T(8,128)S(1)} %get-tuple-element.1204), channel_id=1, source_target_pairs={{0,8},{8,16},{16,24},{24,32},{32,40},{40,48},{48,56},{56,64},{64,7... | collective-permute-start | bytes 110600 | tf_op jit(solution)/shard_map/ppermute | solution.py:17
  110.2 6.4 %collective-permute-done.6 = f32[2,1,512,9]{3,2,1,0:T(8,128)S(1)} collective-permute-done((f32[2,1,512,9]{3,2,1,0:T(8,128)S(1)}, f32[2,1,512,9]{3,2,1,0:T(8,128)S(1)}, u32[]{:S(2)}, u32[]{:S(2)}) %collective-permute-start.6) | collective-permute-done | bytes 36896 | tf_op jit(solution)/shard_map/ppermute | solution.py:17
  116.7 15.2 %collective-permute-done.7 = f32[2,1,512,9]{3,2,1,0:T(8,128)S(1)} collective-permute-done((f32[2,1,512,9]{3,2,1,0:T(8,128)S(1)}, f32[2,1,512,9]{3,2,1,0:T(8,128)S(1)}, u32[]{:S(2)}, u32[]{:S(2)}) %collective-permute-start.7) | collective-permute-done | bytes 36896 | tf_op jit(solution)/shard_map/ppermute | solution.py:18
  132.3 6.6 %while.131 = (s32[]{:T(128)}, f32[1,512,128]{2,1,0:T(8,128)S(1)}, f32[1,512,128]{2,1,0:T(8,128)S(1)}, f32[2,1,19,128]{3,2,1,0:T(8,128)S(1)}, f32[2,1,512,146]{3,2,1,0:T(8,128)S(1)}, /*index=5*/s32[]{:T(128)}, s32[]{:T(128)}, s32[]{}) while((s32[]{:T(128)}, f32[1,512,128]{2,1,0:T(8,128)S(1)}, f32[1,512,128]{2,1,0:T(8,128)S(1)}, ...), condition=%wide.region_12.13_spmd.clone, body=%wide.region_11.12_spmd.clone.sunk | while | flops 655364 | bytes 1576059 | solution.py:55
  139.0 4.2 %collective-permute-start.8 = (f32[2,1,9,128]{3,2,1,0:T(8,128)S(1)}, f32[2,1,9,128]{3,2,1,0:T(8,128)S(1)}, u32[]{:S(2)}, u32[]{:S(2)}) collective-permute-start(f32[2,1,9,128]{3,2,1,0:T(8,128)S(1)} %get-tuple-element.1202), channel_id=1, source_target_pairs={{0,128},{128,256},{256,384},{1,129},{129,257},{257,385},{2,130},{1... | collective-permute-start | bytes 27656 | tf_op jit(solution)/shard_map/ppermute | solution.py:17
  144.7 5.1 %collective-permute-done.9 = f32[2,1,9,128]{3,2,1,0:T(8,128)S(1)} collective-permute-done((f32[2,1,9,128]{3,2,1,0:T(8,128)S(1)}, f32[2,1,9,128]{3,2,1,0:T(8,128)S(1)}, u32[]{:S(2)}, u32[]{:S(2)}) %collective-permute-start.9) | collective-permute-done | bytes 9248 | tf_op jit(solution)/shard_map/ppermute | solution.py:18
  149.8 6.6 %while.132 = (s32[]{:T(128)}, f32[1,512,128]{2,1,0:T(8,128)S(1)}, f32[1,512,128]{2,1,0:T(8,128)S(1)}, f32[2,1,19,512]{3,2,1,0:T(8,128)S(1)}, f32[2,1,530,128]{3,2,1,0:T(8,128)S(1)}, /*index=5*/s32[]{:T(128)}, s32[]{:T(128)}, s32[]{}) while((s32[]{:T(128)}, f32[1,512,128]{2,1,0:T(8,128)S(1)}, f32[1,512,128]{2,1,0:T(8,128)S(1)}, ...), condition=%wide.region_15.16_spmd.clone, body=%wide.region_14.15_spmd.clone.sunk | while | flops 655364 | bytes 1585275 | solution.py:55
  156.4 5.5 %collective-permute-start.10 = (f32[2,1,9,128]{3,2,1,0:T(8,128)S(1)}, f32[2,1,9,128]{3,2,1,0:T(8,128)S(1)}, u32[]{:S(2)}, u32[]{:S(2)}) collective-permute-start(f32[2,1,9,128]{3,2,1,0:T(8,128)S(1)} %get-tuple-element.1200), channel_id=1, source_target_pairs={{0,128},{128,256},{256,384},{1,129},{129,257},{257,385},{2,130},{1... | collective-permute-start | bytes 27656 | tf_op jit(solution)/shard_map/ppermute | solution.py:17
  163.2 4.1 %collective-permute-done.11 = f32[2,1,9,128]{3,2,1,0:T(8,128)S(1)} collective-permute-done((f32[2,1,9,128]{3,2,1,0:T(8,128)S(1)}, f32[2,1,9,128]{3,2,1,0:T(8,128)S(1)}, u32[]{:S(2)}, u32[]{:S(2)}) %collective-permute-start.11) | collective-permute-done | bytes 9248 | tf_op jit(solution)/shard_map/ppermute | solution.py:18
  167.3 6.6 %while.133 = (s32[]{:T(128)}, f32[1,512,128]{2,1,0:T(8,128)S(1)}, f32[1,512,128]{2,1,0:T(8,128)S(1)}, f32[2,1,19,512]{3,2,1,0:T(8,128)S(1)}, f32[2,1,530,128]{3,2,1,0:T(8,128)S(1)}, /*index=5*/s32[]{:T(128)}, s32[]{:T(128)}, s32[]{}) while((s32[]{:T(128)}, f32[1,512,128]{2,1,0:T(8,128)S(1)}, f32[1,512,128]{2,1,0:T(8,128)S(1)}, ...), condition=%wide.region_17.18_spmd.clone, body=%wide.region_16.17_spmd.clone.sunk | while | flops 655364 | bytes 1585275 | solution.py:55
  174.0 3.1 %collective-permute-start.12 = (f32[2,1,9,128]{3,2,1,0:T(8,128)S(1)}, f32[2,1,9,128]{3,2,1,0:T(8,128)S(1)}, u32[]{:S(2)}, u32[]{:S(2)}) collective-permute-start(f32[2,1,9,128]{3,2,1,0:T(8,128)S(1)} %get-tuple-element.1198), channel_id=1, source_target_pairs={{0,128},{128,256},{256,384},{1,129},{129,257},{257,385},{2,130},{1... | collective-permute-start | bytes 27656 | tf_op jit(solution)/shard_map/ppermute | solution.py:17
  178.4 4.1 %collective-permute-done.13 = f32[2,1,9,128]{3,2,1,0:T(8,128)S(1)} collective-permute-done((f32[2,1,9,128]{3,2,1,0:T(8,128)S(1)}, f32[2,1,9,128]{3,2,1,0:T(8,128)S(1)}, u32[]{:S(2)}, u32[]{:S(2)}) %collective-permute-start.13) | collective-permute-done | bytes 9248 | tf_op jit(solution)/shard_map/ppermute | solution.py:18
  182.5 6.6 %while.134 = (s32[]{:T(128)}, f32[1,512,128]{2,1,0:T(8,128)S(1)}, f32[1,512,128]{2,1,0:T(8,128)S(1)}, f32[2,1,19,512]{3,2,1,0:T(8,128)S(1)}, f32[2,1,530,128]{3,2,1,0:T(8,128)S(1)}, /*index=5*/s32[]{:T(128)}, s32[]{:T(128)}, s32[]{}) while((s32[]{:T(128)}, f32[1,512,128]{2,1,0:T(8,128)S(1)}, f32[1,512,128]{2,1,0:T(8,128)S(1)}, ...), condition=%wide.region_19.20_spmd.clone, body=%wide.region_18.19_spmd.clone.sunk | while | flops 655364 | bytes 1585275 | solution.py:55
  189.2 3.1 %collective-permute-start.14 = (f32[2,1,9,128]{3,2,1,0:T(8,128)S(1)}, f32[2,1,9,128]{3,2,1,0:T(8,128)S(1)}, u32[]{:S(2)}, u32[]{:S(2)}) collective-permute-start(f32[2,1,9,128]{3,2,1,0:T(8,128)S(1)} %get-tuple-element.1196), channel_id=1, source_target_pairs={{0,128},{128,256},{256,384},{1,129},{129,257},{257,385},{2,130},{1... | collective-permute-start | bytes 27656 | tf_op jit(solution)/shard_map/ppermute | solution.py:17
  193.7 4.0 %collective-permute-done.15 = f32[2,1,9,128]{3,2,1,0:T(8,128)S(1)} collective-permute-done((f32[2,1,9,128]{3,2,1,0:T(8,128)S(1)}, f32[2,1,9,128]{3,2,1,0:T(8,128)S(1)}, u32[]{:S(2)}, u32[]{:S(2)}) %collective-permute-start.15) | collective-permute-done | bytes 9248 | tf_op jit(solution)/shard_map/ppermute | solution.py:18
  197.7 6.7 %while.135 = (s32[]{:T(128)}, f32[1,512,128]{2,1,0:T(8,128)S(1)}, f32[1,512,128]{2,1,0:T(8,128)S(1)}, f32[2,1,19,512]{3,2,1,0:T(8,128)S(1)}, f32[2,1,530,128]{3,2,1,0:T(8,128)S(1)}, /*index=5*/s32[]{:T(128)}, s32[]{:T(128)}, s32[]{}) while((s32[]{:T(128)}, f32[1,512,128]{2,1,0:T(8,128)S(1)}, f32[1,512,128]{2,1,0:T(8,128)S(1)}, ...), condition=%wide.region_21.22_spmd.clone, body=%wide.region_20.21_spmd.clone.sunk | while | flops 655364 | bytes 1585275 | solution.py:55
  206.3 14.4 %all-to-all-start = ((f32[32,1,128]{2,1,0:T(1,128)}), f32[32,1,128]{2,1,0:T(1,128)S(1)}, u32[]{:S(2)}, u32[]{:S(2)}) async-start(f32[32,1,128]{2,1,0:T(1,128)} %broadcast_in_dim.127), calls=%async_computation | async-start | bytes 32768 | tf_op jit(solution)/shard_map/all_to_all | solution.py:25
  221.5 8.6 %all-to-all-done = f32[32,1,128]{2,1,0:T(1,128)S(1)} async-done(((f32[32,1,128]{2,1,0:T(1,128)}), f32[32,1,128]{2,1,0:T(1,128)S(1)}, u32[]{:S(2)}, u32[]{:S(2)}) %all-to-all-start) | async-done | bytes 16416 | tf_op jit(solution)/shard_map/all_to_all | solution.py:25
  (377 shorter events, 65.2 us)
Async XLA Ops:
  0.6 7.6 %copy-start.2 = (s32[16,8]{0,1:T(8,128)S(1)}, s32[16,8]{0,1:T(8,128)}, u32[]{:S(2)}) copy-start(s32[16,8]{0,1:T(8,128)} %param.25) | copy-start | bytes 1540
  0.6 30.1 %copy-start = (f32[2,1,512,128]{3,2,1,0:T(8,128)S(1)}, f32[2,1,512,128]{3,2,1,0:T(8,128)}, u32[]{:S(2)}) copy-start(f32[2,1,512,128]{3,2,1,0:T(8,128)} %param.22) | copy-start | bytes 1572868
  2.2 6.2 %copy-start.1 = (f32[2,64,19]{1,0,2:T(2,128)S(1)}, f32[2,64,19]{1,0,2:T(2,128)}, u32[]{:S(2)}) copy-start(f32[2,64,19]{1,0,2:T(2,128)} %param.23) | copy-start | bytes 29188
  2.2 11.5 %collective-permute-start = (f32[2,1,512,9]{3,2,1,0:T(8,128)S(1)}, f32[2,1,512,9]{3,2,1,0:T(8,128)S(1)}, u32[]{:S(2)}, u32[]{:S(2)}) collective-permute-start(f32[2,1,512,9]{3,2,1,0:T(8,128)S(1)} %get-tuple-element.1210), channel_id=1, source_target_pairs={{0,8},{8,16},{16,24},{24,32},{32,40},{40,48},{48,56},{56,64},{64,7... | collective-permute-start | bytes 110600 | tf_op jit(solution)/shard_map/ppermute | solution.py:17
  6.3 24.5 %collective-permute-start.1 = (f32[2,1,512,9]{3,2,1,0:T(8,128)S(1)}, f32[2,1,512,9]{3,2,1,0:T(8,128)S(1)}, u32[]{:S(2)}, u32[]{:S(2)}) collective-permute-start(f32[2,1,512,9]{3,2,1,0:T(8,128)S(1)} %get-tuple-element.1211), channel_id=1, source_target_pairs={{8,0},{16,8},{24,16},{32,24},{40,32},{48,40},{56,48},{64,56},{72,6... | collective-permute-start | bytes 110600 | tf_op jit(solution)/shard_map/ppermute | solution.py:18
  8.4 0.7 copy-start.3
  9.2 0.7 copy-start.4
  38.0 12.9 %collective-permute-start.2 = (f32[2,1,512,9]{3,2,1,0:T(8,128)S(1)}, f32[2,1,512,9]{3,2,1,0:T(8,128)S(1)}, u32[]{:S(2)}, u32[]{:S(2)}) collective-permute-start(f32[2,1,512,9]{3,2,1,0:T(8,128)S(1)} %get-tuple-element.1208), channel_id=1, source_target_pairs={{0,8},{8,16},{16,24},{24,32},{32,40},{40,48},{48,56},{56,64},{64,7... | collective-permute-start | bytes 110600 | tf_op jit(solution)/shard_map/ppermute | solution.py:17
  41.3 23.6 %collective-permute-start.3 = (f32[2,1,512,9]{3,2,1,0:T(8,128)S(1)}, f32[2,1,512,9]{3,2,1,0:T(8,128)S(1)}, u32[]{:S(2)}, u32[]{:S(2)}) collective-permute-start(f32[2,1,512,9]{3,2,1,0:T(8,128)S(1)} %get-tuple-element.1209), channel_id=1, source_target_pairs={{8,0},{16,8},{24,16},{32,24},{40,32},{48,40},{56,48},{64,56},{72,6... | collective-permute-start | bytes 110600 | tf_op jit(solution)/shard_map/ppermute | solution.py:18
  72.2 12.1 %collective-permute-start.4 = (f32[2,1,512,9]{3,2,1,0:T(8,128)S(1)}, f32[2,1,512,9]{3,2,1,0:T(8,128)S(1)}, u32[]{:S(2)}, u32[]{:S(2)}) collective-permute-start(f32[2,1,512,9]{3,2,1,0:T(8,128)S(1)} %get-tuple-element.1206), channel_id=1, source_target_pairs={{0,8},{8,16},{16,24},{24,32},{32,40},{40,48},{48,56},{56,64},{64,7... | collective-permute-start | bytes 110600 | tf_op jit(solution)/shard_map/ppermute | solution.py:17
  75.4 22.8 %collective-permute-start.5 = (f32[2,1,512,9]{3,2,1,0:T(8,128)S(1)}, f32[2,1,512,9]{3,2,1,0:T(8,128)S(1)}, u32[]{:S(2)}, u32[]{:S(2)}) collective-permute-start(f32[2,1,512,9]{3,2,1,0:T(8,128)S(1)} %get-tuple-element.1207), channel_id=1, source_target_pairs={{8,0},{16,8},{24,16},{32,24},{40,32},{48,40},{56,48},{64,56},{72,6... | collective-permute-start | bytes 110600 | tf_op jit(solution)/shard_map/ppermute | solution.py:18
  105.5 11.2 %collective-permute-start.6 = (f32[2,1,512,9]{3,2,1,0:T(8,128)S(1)}, f32[2,1,512,9]{3,2,1,0:T(8,128)S(1)}, u32[]{:S(2)}, u32[]{:S(2)}) collective-permute-start(f32[2,1,512,9]{3,2,1,0:T(8,128)S(1)} %get-tuple-element.1204), channel_id=1, source_target_pairs={{0,8},{8,16},{16,24},{24,32},{32,40},{40,48},{48,56},{56,64},{64,7... | collective-permute-start | bytes 110600 | tf_op jit(solution)/shard_map/ppermute | solution.py:17
  108.7 23.1 %collective-permute-start.7 = (f32[2,1,512,9]{3,2,1,0:T(8,128)S(1)}, f32[2,1,512,9]{3,2,1,0:T(8,128)S(1)}, u32[]{:S(2)}, u32[]{:S(2)}) collective-permute-start(f32[2,1,512,9]{3,2,1,0:T(8,128)S(1)} %get-tuple-element.1205), channel_id=1, source_target_pairs={{8,0},{16,8},{24,16},{32,24},{40,32},{48,40},{56,48},{64,56},{72,6... | collective-permute-start | bytes 110600 | tf_op jit(solution)/shard_map/ppermute | solution.py:18
  139.0 5.7 %collective-permute-start.8 = (f32[2,1,9,128]{3,2,1,0:T(8,128)S(1)}, f32[2,1,9,128]{3,2,1,0:T(8,128)S(1)}, u32[]{:S(2)}, u32[]{:S(2)}) collective-permute-start(f32[2,1,9,128]{3,2,1,0:T(8,128)S(1)} %get-tuple-element.1202), channel_id=1, source_target_pairs={{0,128},{128,256},{256,384},{1,129},{129,257},{257,385},{2,130},{1... | collective-permute-start | bytes 27656 | tf_op jit(solution)/shard_map/ppermute | solution.py:17
  143.2 6.6 %collective-permute-start.9 = (f32[2,1,9,128]{3,2,1,0:T(8,128)S(1)}, f32[2,1,9,128]{3,2,1,0:T(8,128)S(1)}, u32[]{:S(2)}, u32[]{:S(2)}) collective-permute-start(f32[2,1,9,128]{3,2,1,0:T(8,128)S(1)} %get-tuple-element.1203), channel_id=1, source_target_pairs={{128,0},{256,128},{384,256},{129,1},{257,129},{385,257},{130,2},{2... | collective-permute-start | bytes 27656 | tf_op jit(solution)/shard_map/ppermute | solution.py:18
  156.4 6.8 %collective-permute-start.10 = (f32[2,1,9,128]{3,2,1,0:T(8,128)S(1)}, f32[2,1,9,128]{3,2,1,0:T(8,128)S(1)}, u32[]{:S(2)}, u32[]{:S(2)}) collective-permute-start(f32[2,1,9,128]{3,2,1,0:T(8,128)S(1)} %get-tuple-element.1200), channel_id=1, source_target_pairs={{0,128},{128,256},{256,384},{1,129},{129,257},{257,385},{2,130},{1... | collective-permute-start | bytes 27656 | tf_op jit(solution)/shard_map/ppermute | solution.py:17
  161.9 5.4 %collective-permute-start.11 = (f32[2,1,9,128]{3,2,1,0:T(8,128)S(1)}, f32[2,1,9,128]{3,2,1,0:T(8,128)S(1)}, u32[]{:S(2)}, u32[]{:S(2)}) collective-permute-start(f32[2,1,9,128]{3,2,1,0:T(8,128)S(1)} %get-tuple-element.1201), channel_id=1, source_target_pairs={{128,0},{256,128},{384,256},{129,1},{257,129},{385,257},{130,2},{2... | collective-permute-start | bytes 27656 | tf_op jit(solution)/shard_map/ppermute | solution.py:18
  174.0 4.5 %collective-permute-start.12 = (f32[2,1,9,128]{3,2,1,0:T(8,128)S(1)}, f32[2,1,9,128]{3,2,1,0:T(8,128)S(1)}, u32[]{:S(2)}, u32[]{:S(2)}) collective-permute-start(f32[2,1,9,128]{3,2,1,0:T(8,128)S(1)} %get-tuple-element.1198), channel_id=1, source_target_pairs={{0,128},{128,256},{256,384},{1,129},{129,257},{257,385},{2,130},{1... | collective-permute-start | bytes 27656 | tf_op jit(solution)/shard_map/ppermute | solution.py:17
  177.1 5.4 %collective-permute-start.13 = (f32[2,1,9,128]{3,2,1,0:T(8,128)S(1)}, f32[2,1,9,128]{3,2,1,0:T(8,128)S(1)}, u32[]{:S(2)}, u32[]{:S(2)}) collective-permute-start(f32[2,1,9,128]{3,2,1,0:T(8,128)S(1)} %get-tuple-element.1199), channel_id=1, source_target_pairs={{128,0},{256,128},{384,256},{129,1},{257,129},{385,257},{130,2},{2... | collective-permute-start | bytes 27656 | tf_op jit(solution)/shard_map/ppermute | solution.py:18
  189.2 4.5 %collective-permute-start.14 = (f32[2,1,9,128]{3,2,1,0:T(8,128)S(1)}, f32[2,1,9,128]{3,2,1,0:T(8,128)S(1)}, u32[]{:S(2)}, u32[]{:S(2)}) collective-permute-start(f32[2,1,9,128]{3,2,1,0:T(8,128)S(1)} %get-tuple-element.1196), channel_id=1, source_target_pairs={{0,128},{128,256},{256,384},{1,129},{129,257},{257,385},{2,130},{1... | collective-permute-start | bytes 27656 | tf_op jit(solution)/shard_map/ppermute | solution.py:17
  192.3 5.4 %collective-permute-start.15 = (f32[2,1,9,128]{3,2,1,0:T(8,128)S(1)}, f32[2,1,9,128]{3,2,1,0:T(8,128)S(1)}, u32[]{:S(2)}, u32[]{:S(2)}) collective-permute-start(f32[2,1,9,128]{3,2,1,0:T(8,128)S(1)} %get-tuple-element.1197), channel_id=1, source_target_pairs={{128,0},{256,128},{384,256},{129,1},{257,129},{385,257},{130,2},{2... | collective-permute-start | bytes 27656 | tf_op jit(solution)/shard_map/ppermute | solution.py:18
  206.3 23.8 %all-to-all-start = ((f32[32,1,128]{2,1,0:T(1,128)}), f32[32,1,128]{2,1,0:T(1,128)S(1)}, u32[]{:S(2)}, u32[]{:S(2)}) async-start(f32[32,1,128]{2,1,0:T(1,128)} %broadcast_in_dim.127), calls=%async_computation | async-start | bytes 32768 | tf_op jit(solution)/shard_map/all_to_all | solution.py:25
where the time goes:
time: 231 us
  waiting for transfers between devices  112 us (48%)
  starting transfers between devices  54.4 us (24%)
  other arithmetic  50.6 us (22%)
  local copies, waits for them, and re-layouts  6.71 us (3%)
  loops' own time  5.23 us (2%)
    ppermute x8, waiting for transfers between devices, extended(): after = lax.ppermute(first, axis, down)  77.4 us
    add x152, other arithmetic, add_tap(): imag_sum = totals[1] + (coef_real * window[1] + coef_imag * window[0])  45.6 us
    ppermute x8, starting transfers between devices, extended(): before = lax.ppermute(last, axis, up)  29.7 us
    ppermute x8, waiting for transfers between devices, extended(): before = lax.ppermute(last, axis, up)  25.6 us
    all_to_all x1, starting transfers between devices, from_everyone(): lax.all_to_all(jnp.broadcast_to(shard[None], (size, *shard.shape)), axis,...  14.4 us
    ppermute x8, starting transfers between devices, extended(): after = lax.ppermute(first, axis, down)  10.3 us
    all_to_all x1, waiting for transfers between devices, from_everyone(): lax.all_to_all(jnp.broadcast_to(shard[None], (size, *shard.shape)), axis,...  8.58 us
    another operation x8, loops' own time, convolve(): lax.fori_loop(0, coefficients.shape[2], add_tap, (zeros_init, zeros_init))  5.23 us
  transfers between devices with their start and end apart: 17, of which 13 were waited for; matrix products, arithmetic and copies ran while one was open for 1% of the time, Pallas kernels for 0%

commit v1 on v0

v1 whole, which is shorter than its diff:
```python
import functools

import jax
import jax.numpy as jnp
from jax import lax
from jax.experimental import pallas as pl
from jax.experimental.pallas import tpu as pltpu
from jax.sharding import PartitionSpec as P

MESH = pl.DeviceIdType.MESH
F32 = jnp.float32
BF = jnp.bfloat16
TILE = 16
TAPS = 19
HALO = 36
BLK = 128
PAD = 64
WIN = 256
SLAB = 72


def split(x):
    hi = x.astype(BF)
    return hi, (x - hi.astype(F32)).astype(BF)


def dot3(ah, al, bh, bl):
    a = jnp.concatenate([ah, al, ah], axis=1)
    b = jnp.concatenate([bh, bh, bl], axis=0)
    return jnp.dot(a, b, preferred_element_type=F32)


def rows(a, b):
    return jnp.concatenate([a, b], axis=0)


def lanes(a, b):
    return jnp.concatenate([a, b], axis=1)


def operator_block(cr, ci):
    ar = pltpu.roll(cr, 0, 1, stride=1, stride_axis=0)
    ai = pltpu.roll(ci, 0, 1, stride=1, stride_axis=0)
    rh, rl = split(ar)
    ih, il = split(ai)
    o = dot3(rows(rh, ih), rows(rl, il), lanes(rh, ih), lanes(rl, il))
    br = o[:WIN, :WIN] - o[WIN:, WIN:]
    bi = o[:WIN, WIN:] + o[WIN:, :WIN]
    rh, rl = split(br)
    ih, il = split(bi)
    mid = slice(PAD, PAD + BLK)
    o = dot3(rows(rh[mid], ih[mid]), rows(rl[mid], il[mid]), lanes(rh, ih), lanes(rl, il))
    return o[:BLK, :WIN] - o[BLK:, WIN:], o[:BLK, WIN:] + o[BLK:, :WIN]


def upper_half():
    return lax.broadcasted_iota(jnp.int32, (8, BLK), 0) >= 4


def pack_last(buf, xr, xi):
    buf[0:32, :] = xr[96:128]
    buf[32:64, :] = xi[96:128]
    buf[64:72, :] = jnp.where(upper_half(), xr[88:96], pltpu.roll(xi[88:96], 4, 0))


def pack_first(buf, xr, xi):
    buf[0:32, :] = xr[0:32]
    buf[32:64, :] = xi[0:32]
    buf[64:72, :] = jnp.where(upper_half(), pltpu.roll(xi[32:40], 4, 0), xr[32:40])


def kernel(
    n_src, n_rcv, n_freq,
    u_ref, op_ref, vel_ref, idx_ref, wgt_ref, perm_ref,
    out_ref, img_ref,
    tab, raw, mix, crw, cw, w_op, s_op, xh, xl,
    to_l, to_r, from_l, from_r, to_u, to_d, from_u, from_d,
    img_mine, img_all, img_sum, img_got,
    r_send, r_recv, s_send, s_recv, f_send, f_recv, g_send, g_recv,
):
    h = lax.axis_index("src")
    c = lax.axis_index("rcv")
    f = lax.axis_index("freq")
    n_blk = out_ref.shape[2] // BLK
    n_tile = vel_ref.shape[0]
    n_vel = idx_ref.shape[0]
    has_l, has_r = c > 0, c < n_rcv - 1
    has_u, has_d = h > 0, h < n_src - 1
    owner = h == c // n_blk

    barrier = pltpu.get_barrier_semaphore()

    @pl.when(has_l)
    def _():
        pl.semaphore_signal(barrier, inc=1, device_id={"rcv": c - 1}, device_id_type=MESH)

    @pl.when(has_r)
    def _():
        pl.semaphore_signal(barrier, inc=1, device_id={"rcv": c + 1}, device_id_type=MESH)

    for d in range(1, n_src):
        pl.semaphore_signal(barrier, inc=1, device_id={"src": lax.rem(h + d, n_src)}, device_id_type=MESH)
    for d in range(1, n_freq):
        pl.semaphore_signal(barrier, inc=1, device_id={"freq": lax.rem(f + d, n_freq)}, device_id_type=MESH)

    def pack_chunk(q, _):
        r = pl.multiple_of(q * BLK, BLK)
        tr = u_ref[0, 0, pl.ds(r, BLK), :].T
        ti = u_ref[1, 0, pl.ds(r, BLK), :].T
        pack_first(to_l.at[q], tr, ti)
        pack_last(to_r.at[q], tr, ti)
        return 0

    lax.fori_loop(0, n_blk, pack_chunk, 0)

    @pl.when(jnp.logical_not(has_l))
    def _():
        from_l[...] = jnp.zeros_like(from_l)

    @pl.when(jnp.logical_not(has_r))
    def _():
        from_r[...] = jnp.zeros_like(from_r)

    @pl.when(jnp.logical_not(has_u))
    def _():
        from_u[...] = jnp.zeros_like(from_u)

    @pl.when(jnp.logical_not(has_d))
    def _():
        from_d[...] = jnp.zeros_like(from_d)

    count = has_l.astype(jnp.int32) + has_r.astype(jnp.int32) + (n_src - 1) + (n_freq - 1)
    pl.semaphore_wait(barrier, count)

    def copy_l(q):
        return pltpu.make_async_remote_copy(
            to_l.at[q], from_r.at[q], r_send.at[0, q], r_recv.at[0, q],
            device_id={"rcv": jnp.maximum(c - 1, 0)}, device_id_type=MESH)

    def copy_r(q):
        return pltpu.make_async_remote_copy(
            to_r.at[q], from_l.at[q], r_send.at[1, q], r_recv.at[1, q],
            device_id={"rcv": jnp.minimum(c + 1, n_rcv - 1)}, device_id_type=MESH)

    def copy_u():
        return pltpu.make_async_remote_copy(
            to_u, from_d, s_send.at[0], s_recv.at[0],
            device_id={"src": jnp.maximum(h - 1, 0)}, device_id_type=MESH)

    def copy_d():
        return pltpu.make_async_remote_copy(
            to_d, from_u, s_send.at[1], s_recv.at[1],
            device_id={"src": jnp.minimum(h + 1, n_src - 1)}, device_id_type=MESH)

    order = [0, n_blk - 1] + list(range(1, n_blk - 1))
    for q in order:
        @pl.when(has_l)
        def _():
            copy_l(q).start()

        @pl.when(has_r)
        def _():
            copy_r(q).start()

    tab[...] = jnp.zeros_like(tab)
    tab[:, :, 0:TAPS] = op_ref[...]
    slot = perm_ref[0]
    for v in range(n_vel):
        i = idx_ref[v, slot]
        wgt = wgt_ref[v, slot]
        for p in range(2):
            raw[p, v:v + 1, :] = tab[p, pl.ds(i, 1), :] * (1.0 - wgt) + tab[p, pl.ds(i + 1, 1), :] * wgt
    for p in range(2):
        wide = lanes(raw[p], jnp.zeros((n_vel, BLK), F32))
        mix[:, WIN * p:WIN * (p + 1)] = pltpu.roll(wide, WIN - TAPS // 2, 1)

    def taps_at(dst, first_tile):
        def one(t, _):
            g = first_tile + t
            inside = jnp.logical_and(g >= 0, g < n_tile).astype(F32)
            v = vel_ref[jnp.clip(g, 0, n_tile - 1)]
            line = mix[pl.ds(v, 1), :] * inside
            dst[pl.ds(pl.multiple_of(t * TILE, TILE), TILE), :] = jnp.broadcast_to(line, (TILE, 2 * WIN))
            return 0
        lax.fori_loop(0, dst.shape[0] // TILE, one, 0)

    taps_at(crw, (c * BLK - PAD) // TILE)
    mr, mi = operator_block(crw[:, :WIN], crw[:, WIN:])
    sub = upper_half()
    pieces = []
    for m in (mr, mi):
        mt = lanes(m[:, :BLK], m[:, BLK:])
        t = rows(mt[:, :BLK].T, mt[:, BLK:].T)
        pieces.append(jnp.concatenate([
            t[PAD:PAD + BLK], t[32:64], t[192:224], jnp.where(sub, t[24:32], t[224:232]),
            jnp.zeros((BLK - SLAB, BLK), F32)], axis=0))
    wh, wl = split(lanes(pieces[0], pieces[1]))
    w_op[0:WIN, :] = wh
    w_op[WIN:2 * WIN, :] = wh
    w_op[2 * WIN:, :] = wl

    def receivers(q):
        @pl.when(has_r)
        def _():
            copy_l(q).wait_recv()

        @pl.when(has_l)
        def _():
            copy_r(q).wait_recv()

        l8, r8 = from_l[q, 64:72, :], from_r[q, 64:72, :]
        zero = jnp.zeros((BLK - SLAB, BLK), F32)
        hr = jnp.concatenate([from_l[q, 0:32, :], from_r[q, 0:32, :], jnp.where(sub, l8, r8), zero], axis=0).T
        hi = jnp.concatenate([from_l[q, 32:64, :], from_r[q, 32:64, :],
                              pltpu.roll(jnp.where(sub, r8, l8), 4, 0), zero], axis=0).T
        at = slice(q * BLK, (q + 1) * BLK)
        a = rows(lanes(u_ref[0, 0, at, :], hr), lanes(u_ref[1, 0, at, :], hi))
        ah, al = split(a)
        o = jnp.dot(jnp.concatenate([ah, al, ah], axis=1), w_op[...], preferred_element_type=F32)
        xr = o[:BLK, :BLK] - o[BLK:, BLK:]
        xi = o[:BLK, BLK:] + o[BLK:, :BLK]
        xhi, xlo = split(lanes(xr, xi))
        xh[PAD + q * BLK:PAD + (q + 1) * BLK, :] = xhi
        xl[PAD + q * BLK:PAD + (q + 1) * BLK, :] = xlo
        return xr, xi

    xr, xi = receivers(order[0])
    pack_first(to_u, xr, xi)

    @pl.when(has_u)
    def _():
        copy_u().start()

    xr, xi = receivers(order[1])
    pack_last(to_d, xr, xi)

    @pl.when(has_d)
    def _():
        copy_d().start()

    taps_at(cw, (h * n_blk * BLK - PAD) // TILE)

    def make_source_operator(b, _):
        r = pl.multiple_of(b * BLK, BLK)
        sr, si = operator_block(cw[pl.ds(r, WIN), :WIN], cw[pl.ds(r, WIN), WIN:])
        sh, sl = split(rows(sr, si))
        s_op[b, :, :WIN] = sh
        s_op[b, :, WIN:] = sl
        return 0

    lax.fori_loop(0, n_blk, make_source_operator, 0)

    for q in order[2:]:
        receivers(q)

    @pl.when(has_u)
    def _():
        copy_d().wait_recv()

    @pl.when(has_d)
    def _():
        copy_u().wait_recv()

    zero = jnp.zeros((8, BLK), F32)
    u8, d8 = from_u[64:72, :], from_d[64:72, :]
    pad = jnp.zeros((24, 2 * BLK), F32)
    top = jnp.concatenate([
        pad,
        lanes(jnp.where(sub, u8, zero), pltpu.roll(jnp.where(sub, zero, u8), 4, 0)),
        lanes(from_u[0:32, :], from_u[32:64, :])], axis=0)
    low = jnp.concatenate([
        lanes(from_d[0:32, :], from_d[32:64, :]),
        lanes(jnp.where(sub, zero, d8), pltpu.roll(jnp.where(sub, d8, zero), 4, 0)),
        pad], axis=0)
    end = PAD + n_blk * BLK
    xh[0:PAD, :], xl[0:PAD, :] = split(top)
    xh[end:end + PAD, :], xl[end:end + PAD, :] = split(low)

    def sources(b, _):
        r = pl.multiple_of(b * BLK, BLK)
        bh, bl = xh[pl.ds(r, WIN), :], xl[pl.ds(r, WIN), :]
        o = dot3(s_op[b, :, :WIN], s_op[b, :, WIN:], bh, bl)
        out_ref[0, 0, pl.ds(r, BLK), :] = o[:BLK, :BLK] - o[BLK:, BLK:]
        out_ref[1, 0, pl.ds(r, BLK), :] = o[:BLK, BLK:] + o[BLK:, :BLK]
        return 0

    lax.fori_loop(0, n_blk, sources, 0)

    def copy_f(d):
        return pltpu.make_async_remote_copy(
            img_mine, img_all.at[f], f_send.at[d - 1], f_recv.at[d - 1],
            device_id={"freq": lax.rem(f + d, n_freq)}, device_id_type=MESH)

    def copy_g(d):
        return pltpu.make_async_remote_copy(
            img_sum, img_got, g_send.at[d - 1], g_recv,
            device_id={"src": lax.rem(h + d, n_src)}, device_id_type=MESH)

    @pl.when(owner)
    def _():
        r = pl.multiple_of(lax.rem(c, n_blk) * BLK, BLK)
        block = out_ref[0, 0, pl.ds(r, BLK), :]
        on = lax.broadcasted_iota(jnp.int32, (BLK, BLK), 0) == lax.broadcasted_iota(jnp.int32, (BLK, BLK), 1)
        diag = jnp.broadcast_to(jnp.sum(jnp.where(on, block, 0.0), axis=0, keepdims=True), (8, BLK))
        img_mine[...] = diag
        img_all[f] = diag
        for d in range(1, n_freq):
            copy_f(d).start()
        for d in range(1, n_freq):
            copy_f(d).wait()
        total = img_all[0]
        for i in range(1, n_freq):
            total = total + img_all[i]
        img_sum[...] = total
        img_ref[...] = total[0:1]
        for d in range(1, n_src):
            copy_g(d).start()
        for d in range(1, n_src):
            copy_g(d).wait_send()

    @pl.when(jnp.logical_not(owner))
    def _():
        copy_g(1).wait_recv()
        img_ref[...] = img_got[0:1, :]

    for q in order:
        @pl.when(has_l)
        def _():
            copy_l(q).wait_send()

        @pl.when(has_r)
        def _():
            copy_r(q).wait_send()

    @pl.when(has_u)
    def _():
        copy_u().wait_send()

    @pl.when(has_d)
    def _():
        copy_d().wait_send()


def body(n_src, n_rcv, n_freq, wavefield, op_table, vel_index, interp_index, interp_weight, freq_perm):
    n_blk = wavefield.shape[2] // BLK
    n_tab, n_vel = op_table.shape[1], interp_index.shape[0]
    vmem = pl.BlockSpec(memory_space=pltpu.VMEM)
    smem = pl.BlockSpec(memory_space=pltpu.SMEM)
    dma = pltpu.SemaphoreType.DMA
    slabs = [pltpu.VMEM((n_blk, SLAB, BLK), F32)] * 4 + [pltpu.VMEM((SLAB, BLK), F32)] * 4
    sunk, image = pl.pallas_call(
        functools.partial(kernel, n_src, n_rcv, n_freq),
        out_shape=(jax.ShapeDtypeStruct(wavefield.shape, F32), jax.ShapeDtypeStruct((1, BLK), F32)),
        in_specs=[vmem, vmem, smem, smem, smem, smem],
        out_specs=(vmem, vmem),
        scratch_shapes=[
            pltpu.VMEM((2, n_tab, BLK), F32),
            pltpu.VMEM((2, n_vel, BLK), F32),
            pltpu.VMEM((n_vel, 2 * WIN), F32),
            pltpu.VMEM((WIN, 2 * WIN), F32),
            pltpu.VMEM((2 * PAD + n_blk * BLK, 2 * WIN), F32),
            pltpu.VMEM((3 * WIN, WIN), BF),
            pltpu.VMEM((n_blk, WIN, 2 * WIN), BF),
            pltpu.VMEM((2 * PAD + n_blk * BLK, WIN), BF),
            pltpu.VMEM((2 * PAD + n_blk * BLK, WIN), BF),
            *slabs,
            pltpu.VMEM((8, BLK), F32),
            pltpu.VMEM((n_freq, 8, BLK), F32),
            pltpu.VMEM((8, BLK), F32),
            pltpu.VMEM((8, BLK), F32),
            dma((2, n_blk)), dma((2, n_blk)), dma((2,)), dma((2,)),
            dma((max(n_freq - 1, 1),)), dma((max(n_freq - 1, 1),)), dma((max(n_src - 1, 1),)), dma,
        ],
        compiler_params=pltpu.CompilerParams(collective_id=0, has_side_effects=True),
        name="depth_step",
    )(wavefield, op_table, vel_index, interp_index, interp_weight, freq_perm)
    return sunk, image.reshape(BLK)


def solution(mesh):
    sizes = [mesh.shape[a] for a in ("src", "rcv", "freq")]
    in_specs = (P(None, "freq", "src", "rcv"), P(), P(), P(), P(), P("freq"))
    out_specs = (P(None, "freq", "src", "rcv"), P("rcv"))
    return jax.shard_map(functools.partial(body, *sizes), mesh=mesh, in_specs=in_specs, out_specs=out_specs,
                         check_vma=False)
```

time: 231 us -> 40.3 us (0.17)
  the two profiles are of different devices: /device:TPU:1 before, /device:TPU:256 now
where the time goes in v1:
time: 40.3 us; the launch traced here: 40 us
  Pallas kernels  32.9 us (82%)
  local copies, waits for them, and re-layouts  5.82 us (14%)
  between operations  1.31 us (3%)
    pallas_call x1, Pallas kernels, body(): pl.pallas_call(functools.partial(kernel, n_src, n_rcv, n_freq), out_shape...  32.9 us
    unnamed x9, local copies, waits for them, and re-layouts  5.82 us

profile of v1, /device:TPU:256, one launch (start us, length us, event | category | flops | bytes accessed | tf_op | source)
XLA Modules:
  0.0 40.0 jit_solution(16314731249995539026)
XLA Ops:
  0.6 0.0 copy-start
  1.3 1.4 %copy.9.idx_ref = s32[16,8]{1,0:T(8,128)} copy(s32[16,8]{0,1:T(8,128)} %param.9) | data formatting | bytes 1024 | tf_op args[3]
  2.6 1.4 %copy.10.wgt_ref = f32[16,8]{1,0:T(8,128)} copy(f32[16,8]{0,1:T(8,128)} %param.10) | data formatting | bytes 1024 | tf_op args[4]
  4.0 0.0 copy-done
  4.0 0.7 %copy.8.op_ref = f32[2,64,19]{2,1,0:T(8,128)} copy(f32[2,64,19]{1,0,2:T(2,128)S(1)} %copy-done) | data formatting | bytes 19456 | tf_op args[1]
  4.7 32.9 %depth_step.1 = (f32[2,1,512,128]{3,2,1,0:T(8,128)}, f32[1,128]{1,0:T(1,128)}) custom-call(f32[2,1,512,128]{3,2,1,0:T(8,128)} %u_ref.1, f32[2,64,19]{2,1,0:T(8,128)} %copy.8.op_ref, s32[128]{0:T(128)} %vel_ref.1, s32[16,8]{1,0:T(8,128)} %copy.9.idx_ref, f32[16,8]{1,0:T(8,128)} %copy.10.wgt_ref, s32[1]{0:T(128)S(6)} %copy.13.perm_ref), custom_call_target="tpu_custom_call" | custom-call | tf_op jit(solution)/shard_map/depth_step/pallas_call | solution.py:351
  37.6 0.0 copy-start.1
  37.6 1.9 %copy.14 = f32[2,1,512,128]{3,2,1,0:T(8,128)} copy(f32[2,1,512,128]{3,2,1,0:T(8,128)} %get-tuple-element.8) | data formatting | bytes 1048576
  39.5 0.0 copy-done.1
  39.5 0.5 %copy.15 = f32[128]{0:T(128)} copy(f32[128]{0:T(128)S(1)} %bitcast.1) | data formatting | bytes 1024
Async XLA Ops:
  0.6 3.4 %copy-start = (f32[2,64,19]{1,0,2:T(2,128)S(1)}, f32[2,64,19]{1,0,2:T(2,128)}, u32[]{:S(2)}) copy-start(f32[2,64,19]{1,0,2:T(2,128)} %param.7) | copy-start | bytes 29188
  37.6 1.9 %copy-start.1 = (f32[1,128]{1,0:T(1,128)S(1)}, f32[1,128]{1,0:T(1,128)}, u32[]{:S(2)}) copy-start(f32[1,128]{1,0:T(1,128)} %get-tuple-element.5) | copy-start | bytes 1540

commit v2 on v1

v2 whole, which is shorter than its diff:
```python
import functools

import jax
import jax.numpy as jnp
from jax import lax
from jax.experimental import pallas as pl
from jax.experimental.pallas import tpu as pltpu
from jax.sharding import PartitionSpec as P

MESH = pl.DeviceIdType.MESH
F32 = jnp.float32
BF = jnp.bfloat16
TILE = 16
TAPS = 19
HALO = 36
BLK = 128
PAD = 64
WIN = 256
HOLD = 2
SLAB = 72


def split(x):
    hi = x.astype(BF)
    return hi, (x - hi.astype(F32)).astype(BF)


def dot3(ah, al, bh, bl):
    a = jnp.concatenate([ah, al, ah], axis=1)
    b = jnp.concatenate([bh, bh, bl], axis=0)
    return jnp.dot(a, b, preferred_element_type=F32)


def rows(a, b):
    return jnp.concatenate([a, b], axis=0)


def lanes(a, b):
    return jnp.concatenate([a, b], axis=1)


def operator_block(cr, ci):
    ar = pltpu.roll(cr, 0, 1, stride=1, stride_axis=0)
    ai = pltpu.roll(ci, 0, 1, stride=1, stride_axis=0)
    rh, rl = split(ar)
    ih, il = split(ai)
    near = slice(PAD // 2, WIN - PAD // 2)
    o = dot3(rows(rh[near], ih[near]), rows(rl[near], il[near]), lanes(rh, ih), lanes(rl, il))
    n = WIN - PAD
    br = o[:n, :WIN] - o[n:, WIN:]
    bi = o[:n, WIN:] + o[n:, :WIN]
    rh, rl = split(br)
    ih, il = split(bi)
    mid = slice(PAD // 2, PAD // 2 + BLK)
    edge = jnp.zeros((PAD // 2, 2 * WIN), BF)
    bh = jnp.concatenate([edge, lanes(rh, ih), edge], axis=0)
    bl = jnp.concatenate([edge, lanes(rl, il), edge], axis=0)
    o = dot3(rows(rh[mid], ih[mid]), rows(rl[mid], il[mid]), bh, bl)
    return o[:BLK, :WIN] - o[BLK:, WIN:], o[:BLK, WIN:] + o[BLK:, :WIN]


def upper_half():
    return lax.broadcasted_iota(jnp.int32, (8, BLK), 0) >= 4


def pack_last(buf, xr, xi):
    buf[0:32, :] = xr[96:128]
    buf[32:64, :] = xi[96:128]
    buf[64:72, :] = jnp.where(upper_half(), xr[88:96], pltpu.roll(xi[88:96], 4, 0))


def pack_first(buf, xr, xi):
    buf[0:32, :] = xr[0:32]
    buf[32:64, :] = xi[0:32]
    buf[64:72, :] = jnp.where(upper_half(), pltpu.roll(xi[32:40], 4, 0), xr[32:40])


def kernel(
    n_src, n_rcv, n_freq,
    u_ref, op_ref, vel_ref, idx_ref, wgt_ref, perm_ref,
    out_ref, img_ref,
    raw, turn, mix, crw, cw, w_op, s_op, xh, xl,
    to_l, to_r, from_l, from_r, to_u, to_d, from_u, from_d,
    img_mine, img_all,
    r_send, r_recv, s_send, s_recv, f_send, f_recv, known_u, known_d,
):
    h = lax.axis_index("src")
    c = lax.axis_index("rcv")
    f = lax.axis_index("freq")
    n_blk = out_ref.shape[2] // BLK
    n_tile = vel_ref.shape[0]
    n_tab = op_ref.shape[2]
    n_vel = idx_ref.shape[1]
    has_l, has_r = c > 0, c < n_rcv - 1
    has_u, has_d = h > 0, h < n_src - 1
    owner = h == c // n_blk
    quarter = lax.rem(c, n_blk)

    def to(axis, index):
        return dict(device_id={axis: index}, device_id_type=MESH)

    up, down = to("src", jnp.maximum(h - 1, 0)), to("src", jnp.minimum(h + 1, n_src - 1))
    left, right = to("rcv", jnp.maximum(c - 1, 0)), to("rcv", jnp.minimum(c + 1, n_rcv - 1))

    def each(pairs):
        for cond, act in pairs:
            pl.when(cond)(act)

    barrier = pltpu.get_barrier_semaphore()
    each([
        (has_l, lambda: pl.semaphore_signal(barrier, 1, **left)),
        (has_r, lambda: pl.semaphore_signal(barrier, 1, **right)),
        (has_u, lambda: pl.semaphore_signal(barrier, 1, **up)),
        (has_d, lambda: pl.semaphore_signal(barrier, 1, **down)),
    ])
    for d in range(1, n_freq):
        pl.semaphore_signal(barrier, 1, **to("freq", lax.rem(f + d, n_freq)))

    n_mid = n_blk - 1

    def chunk_start(p, col):
        back = lax.rem(col, n_blk) >= n_blk // 2
        return pl.multiple_of(PAD + BLK * jnp.where(back, n_mid - p, p - 1), PAD)

    def part_lines(part, p, col):
        if p == 0:
            last = u_ref.shape[2] - PAD
            return rows(u_ref[part, 0, 0:PAD, :], u_ref[part, 0, last:last + PAD, :])
        return u_ref[part, 0, pl.ds(chunk_start(p, col), BLK), :]

    def pack(p):
        pack_first(to_l.at[p], part_lines(0, p, jnp.maximum(c - 1, 0)).T, part_lines(1, p, jnp.maximum(c - 1, 0)).T)
        pack_last(to_r.at[p], part_lines(0, p, c + 1).T, part_lines(1, p, c + 1).T)

    def copy_l(p):
        return pltpu.make_async_remote_copy(to_l.at[p], from_r.at[p], r_send.at[0, p], r_recv.at[0, p], **left)

    def copy_r(p):
        return pltpu.make_async_remote_copy(to_r.at[p], from_l.at[p], r_send.at[1, p], r_recv.at[1, p], **right)

    def copy_u():
        return pltpu.make_async_remote_copy(to_u, from_d, s_send.at[0], s_recv.at[0], **up)

    def copy_d():
        return pltpu.make_async_remote_copy(to_d, from_u, s_send.at[1], s_recv.at[1], **down)

    def send(p):
        each([(has_l, lambda: copy_l(p).start()), (has_r, lambda: copy_r(p).start())])

    def clear(ref):
        ref[...] = jnp.zeros_like(ref)

    pack(0)
    pack(1)
    each([
        (jnp.logical_not(has_l), lambda: clear(from_l)),
        (jnp.logical_not(has_r), lambda: clear(from_r)),
        (jnp.logical_not(has_u), lambda: clear(from_u)),
        (jnp.logical_not(has_d), lambda: clear(from_d)),
    ])

    clear(raw)
    clear(turn)
    raw[0, 0:TAPS, :] = op_ref[:, 0, :]
    raw[1, 0:TAPS, :] = op_ref[:, 1, :]
    slot = perm_ref[0]
    row = idx_ref[pl.ds(slot, 1), :]
    wgt = wgt_ref[pl.ds(slot, 1), :]
    line = lax.broadcasted_iota(jnp.int32, (n_tab, n_vel), 0)
    table = rows(raw[0], raw[1])
    hi, rest = table.astype(BF), table - table.astype(BF).astype(F32)
    mid, low = split(rest)
    table = jnp.concatenate([hi, mid, low], axis=1)

    def picked(which):
        one = (line == which).astype(F32).astype(BF)
        return jnp.dot(table, jnp.concatenate([one, one, one], axis=0), preferred_element_type=F32)

    turn[0:64, 0:n_vel] = picked(row) * (1.0 - wgt) + picked(row + 1) * wgt
    turned = turn[...].T[0:n_vel]
    few = lax.broadcasted_iota(jnp.int32, (n_vel, BLK), 1) < 32
    none = jnp.zeros((n_vel, BLK), F32)
    for p in range(2):
        part = jnp.where(few, pltpu.roll(turned, (BLK - 32 * p) % BLK, 1), 0.0)
        mix[:, WIN * p:WIN * (p + 1)] = pltpu.roll(lanes(part, none), WIN - TAPS // 2, 1)

    ones = lambda cond: cond.astype(jnp.int32)
    pl.semaphore_wait(barrier, ones(has_l) + ones(has_r) + ones(has_u) + ones(has_d) + (n_freq - 1))
    for p in range(HOLD):
        send(p)

    def tell(t):
        each([
            (has_d if t == 0 else jnp.logical_and(has_d, h >= t), lambda: pl.semaphore_signal(known_u.at[t], 1, **down)),
            (has_u if t == 0 else jnp.logical_and(has_u, h <= n_src - 1 - t),
             lambda: pl.semaphore_signal(known_d.at[t], 1, **up)),
        ])

    def learn(t):
        each([
            (h >= t + 1, lambda: pl.semaphore_wait(known_u.at[t], 1)),
            (h <= n_src - 2 - t, lambda: pl.semaphore_wait(known_d.at[t], 1)),
        ])

    tell(0)
    for p in range(2, n_blk):
        pack(p)

    def taps_at(dst, first_tile):
        def one(t, _):
            g = first_tile + t
            inside = jnp.logical_and(g >= 0, g < n_tile).astype(F32)
            v = vel_ref[jnp.clip(g, 0, n_tile - 1)]
            line = mix[pl.ds(v, 1), :] * inside
            dst[pl.ds(pl.multiple_of(t * TILE, TILE), TILE), :] = jnp.broadcast_to(line, (TILE, 2 * WIN))
            return 0
        lax.fori_loop(0, dst.shape[0] // TILE, one, 0)

    sub = upper_half()
    taps_at(crw, (c * BLK - PAD) // TILE)
    mr, mi = operator_block(crw[:, :WIN], crw[:, WIN:])
    pieces = []
    for m in (mr, mi):
        t = rows(m[:, :BLK].T, m[:, BLK:].T)
        pieces.append(jnp.concatenate([
            t[PAD:PAD + BLK], t[32:64], t[192:224], jnp.where(sub, t[24:32], t[224:232]),
            jnp.zeros((BLK - SLAB, BLK), F32)], axis=0))
    wh, wl = split(lanes(pieces[0], pieces[1]))
    w_op[0:WIN, :] = wh
    w_op[WIN:2 * WIN, :] = wh
    w_op[2 * WIN:, :] = wl
    taps_at(cw, (h * n_blk * BLK - PAD) // TILE)

    def make_source_operator(k):
        b = lax.rem(quarter + k, n_blk)
        r = pl.multiple_of(b * BLK, BLK)
        sr, si = operator_block(cw[pl.ds(r, WIN), :WIN], cw[pl.ds(r, WIN), WIN:])
        sh, sl = split(rows(sr, si))
        s_op[b, :, :WIN] = sh
        s_op[b, :, WIN:] = sl

    def receivers(p):
        each([(has_r, lambda: copy_l(p).wait_recv()), (has_l, lambda: copy_r(p).wait_recv())])
        l8, r8 = from_l[p, 64:72, :], from_r[p, 64:72, :]
        zero = jnp.zeros((BLK - SLAB, BLK), F32)
        hr = jnp.concatenate([from_l[p, 0:32, :], from_r[p, 0:32, :], jnp.where(sub, l8, r8), zero], axis=0).T
        hi = jnp.concatenate([from_l[p, 32:64, :], from_r[p, 32:64, :],
                              pltpu.roll(jnp.where(sub, r8, l8), 4, 0), zero], axis=0).T
        ah, al = split(rows(lanes(part_lines(0, p, c), hr), lanes(part_lines(1, p, c), hi)))
        o = jnp.dot(jnp.concatenate([ah, al, ah], axis=1), w_op[...], preferred_element_type=F32)
        xr = o[:BLK, :BLK] - o[BLK:, BLK:]
        xi = o[:BLK, BLK:] + o[BLK:, :BLK]
        xhi, xlo = split(lanes(xr, xi))
        if p == 0:
            end = n_blk * BLK
            xh[PAD:2 * PAD, :], xl[PAD:2 * PAD, :] = xhi[:PAD], xlo[:PAD]
            xh[end:end + PAD, :], xl[end:end + PAD, :] = xhi[PAD:], xlo[PAD:]
            pack_first(to_u, xr, xi)
            pack_last(to_d, xr, xi)
        else:
            at = pl.ds(chunk_start(p, c) + PAD, BLK)
            xh[at, :] = xhi
            xl[at, :] = xlo

    make_source_operator(0)
    receivers(0)
    each([(has_u, lambda: copy_u().start()), (has_d, lambda: copy_d().start())])
    for p in range(HOLD, n_blk):
        send(p)
    for t in range(1, n_src - 1):
        learn(t - 1)
        tell(t)
    make_source_operator(1)
    receivers(1)
    make_source_operator(2)
    receivers(2)

    each([(has_u, lambda: copy_d().wait_recv()), (has_d, lambda: copy_u().wait_recv())])
    zero = jnp.zeros((8, BLK), F32)
    u8, d8 = from_u[64:72, :], from_d[64:72, :]
    pad = jnp.zeros((24, 2 * BLK), F32)
    top = jnp.concatenate([
        pad,
        lanes(jnp.where(sub, u8, zero), pltpu.roll(jnp.where(sub, zero, u8), 4, 0)),
        lanes(from_u[0:32, :], from_u[32:64, :])], axis=0)
    low = jnp.concatenate([
        lanes(from_d[0:32, :], from_d[32:64, :]),
        lanes(jnp.where(sub, zero, d8), pltpu.roll(jnp.where(sub, d8, zero), 4, 0)),
        pad], axis=0)
    end = PAD + n_blk * BLK
    xh[0:PAD, :], xl[0:PAD, :] = split(top)
    xh[end:end + PAD, :], xl[end:end + PAD, :] = split(low)

    def sources(k):
        b = lax.rem(quarter + k, n_blk)
        r = pl.multiple_of(b * BLK, BLK)
        o = dot3(s_op[b, :, :WIN], s_op[b, :, WIN:], xh[pl.ds(r, WIN), :], xl[pl.ds(r, WIN), :])
        yr = o[:BLK, :BLK] - o[BLK:, BLK:]
        out_ref[0, 0, pl.ds(r, BLK), :] = yr
        out_ref[1, 0, pl.ds(r, BLK), :] = o[:BLK, BLK:] + o[BLK:, :BLK]
        return yr

    n_peer = n_src * n_freq

    def copy_image(d):
        e = lax.rem(h * n_freq + f + d, n_peer)
        return pltpu.make_async_remote_copy(
            img_mine, img_all.at[f], f_send.at[d], f_recv.at[f],
            device_id={"src": e // n_freq, "freq": lax.rem(e, n_freq)}, device_id_type=MESH)

    yr = sources(0)
    learn(n_src - 2)

    @pl.when(owner)
    def _():
        on = lax.broadcasted_iota(jnp.int32, (BLK, BLK), 0) == lax.broadcasted_iota(jnp.int32, (BLK, BLK), 1)
        diag = jnp.broadcast_to(jnp.sum(jnp.where(on, yr, 0.0), axis=0, keepdims=True), (8, BLK))
        img_mine[...] = diag
        img_all[f] = diag

        def start(d, _):
            copy_image(d).start()
            return 0
        lax.fori_loop(1, n_peer, start, 0)

    make_source_operator(3)
    receivers(3)
    for k in range(1, n_blk):
        sources(k)

    def got(i, _):
        @pl.when(jnp.logical_not(jnp.logical_and(owner, f == i)))
        def _():
            pltpu.make_async_remote_copy(
                img_mine, img_all.at[i], f_send.at[0], f_recv.at[i],
                device_id={"src": h, "freq": f}, device_id_type=MESH).wait_recv()
        return 0
    lax.fori_loop(0, n_freq, got, 0)
    total = img_all[0]
    for i in range(1, n_freq):
        total = total + img_all[i]
    img_ref[...] = total[0:1]

    @pl.when(owner)
    def _():
        def sent(d, _):
            copy_image(d).wait_send()
            return 0
        lax.fori_loop(1, n_peer, sent, 0)

    for p in range(n_blk):
        each([(has_l, lambda: copy_l(p).wait_send()), (has_r, lambda: copy_r(p).wait_send())])
    each([(has_u, lambda: copy_u().wait_send()), (has_d, lambda: copy_d().wait_send())])


def body(n_src, n_rcv, n_freq, wavefield, op_table, vel_index, interp_index, interp_weight, freq_perm):
    n_blk = wavefield.shape[2] // BLK
    n_tab, n_vel = op_table.shape[1], interp_index.shape[0]
    vmem = pl.BlockSpec(memory_space=pltpu.VMEM)
    smem = pl.BlockSpec(memory_space=pltpu.SMEM)
    dma, flag = pltpu.SemaphoreType.DMA, pltpu.SemaphoreType.REGULAR
    slabs = [pltpu.VMEM((n_blk, SLAB, BLK), F32)] * 4 + [pltpu.VMEM((SLAB, BLK), F32)] * 4
    length = 2 * PAD + n_blk * BLK
    sunk, image = pl.pallas_call(
        functools.partial(kernel, n_src, n_rcv, n_freq),
        out_shape=(pltpu.VMEM(wavefield.shape, F32), pltpu.VMEM((1, BLK), F32)),
        in_specs=[vmem, vmem, smem, vmem, vmem, smem],
        out_specs=(vmem, vmem),
        scratch_shapes=[
            pltpu.VMEM((2, 32, n_tab), F32),
            pltpu.VMEM((BLK, BLK), F32),
            pltpu.VMEM((n_vel, 2 * WIN), F32),
            pltpu.VMEM((WIN, 2 * WIN), F32),
            pltpu.VMEM((length, 2 * WIN), F32),
            pltpu.VMEM((3 * WIN, WIN), BF),
            pltpu.VMEM((n_blk, WIN, 2 * WIN), BF),
            pltpu.VMEM((length, WIN), BF),
            pltpu.VMEM((length, WIN), BF),
            *slabs,
            pltpu.VMEM((8, BLK), F32),
            pltpu.VMEM((n_freq, 8, BLK), F32),
            dma((2, n_blk)), dma((2, n_blk)), dma((2,)), dma((2,)),
            dma((n_src * n_freq,)), dma((n_freq,)), flag((n_src - 1,)), flag((n_src - 1,)),
        ],
        compiler_params=pltpu.CompilerParams(collective_id=0, has_side_effects=True),
        name="depth_step",
    )(wavefield, jnp.transpose(op_table, (2, 0, 1)), vel_index, interp_index.T, interp_weight.T, freq_perm)
    return sunk, image.reshape(BLK)


def solution(mesh):
    sizes = [mesh.shape[a] for a in ("src", "rcv", "freq")]
    in_specs = (P(None, "freq", "src", "rcv"), P(), P(), P(), P(), P("freq"))
    out_specs = (P(None, "freq", "src", "rcv"), P("rcv"))
    return jax.shard_map(functools.partial(body, *sizes), mesh=mesh, in_specs=in_specs, out_specs=out_specs,
                         check_vma=False)
```

time: 40.3 us -> 28.7 us (0.71)
  the two profiles are of different devices: /device:TPU:256 before, /device:TPU:257 now
where the time goes in v2:
time: 28.7 us; the launch traced here: 28.6 us
  Pallas kernels  26 us (91%)
  local copies, waits for them, and re-layouts  1.31 us (5%)
  between operations  1.29 us (4%)
    pallas_call x1, Pallas kernels, body(): pl.pallas_call(functools.partial(kernel, n_src, n_rcv, n_freq), out_shape...  26 us
    unnamed x2, local copies, waits for them, and re-layouts  1.31 us

profile of v2, /device:TPU:257, one launch (start us, length us, event | category | flops | bytes accessed | tf_op | source)
XLA Modules:
  0.0 28.6 jit_solution(7127251633618007207)
XLA Ops:
  1.3 26.0 %depth_step.1 = (f32[2,1,512,128]{3,2,1,0:T(8,128)S(1)}, f32[1,128]{1,0:T(1,128)S(1)}) custom-call(f32[2,1,512,128]{3,2,1,0:T(8,128)} %u_ref.1, f32[19,2,64]{2,1,0:T(2,128)} %bitcast.5, s32[128]{0:T(128)} %vel_ref.1, s32[8,16]{1,0:T(8,128)} %bitcast.6, f32[8,16]{1,0:T(8,128)} %bitcast.7, s32[1]{0:T(128)S(6)} %copy.12.perm_ref), custom_call_target="tpu_custom_call" | custom-call | tf_op jit(solution)/shard_map/depth_step/pallas_call | solution.py:364
  27.3 0.8 %copy.10 = f32[2,1,512,128]{3,2,1,0:T(8,128)} copy(f32[2,1,512,128]{3,2,1,0:T(8,128)S(1)} %get-tuple-element.6) | data formatting | bytes 1048576
  28.1 0.5 %copy.11 = f32[128]{0:T(128)} copy(f32[128]{0:T(128)S(1)} %bitcast.4) | data formatting | bytes 1024

commit v3 on v2

--- a/solution.py
+++ b/solution.py
@@ -39,24 +39,25 @@
     return jnp.concatenate([a, b], axis=1)
 
 
-def operator_block(cr, ci):
-    ar = pltpu.roll(cr, 0, 1, stride=1, stride_axis=0)
-    ai = pltpu.roll(ci, 0, 1, stride=1, stride_axis=0)
-    rh, rl = split(ar)
-    ih, il = split(ai)
-    near = slice(PAD // 2, WIN - PAD // 2)
-    o = dot3(rows(rh[near], ih[near]), rows(rl[near], il[near]), lanes(rh, ih), lanes(rl, il))
-    n = WIN - PAD
-    br = o[:n, :WIN] - o[n:, WIN:]
-    bi = o[:n, WIN:] + o[n:, :WIN]
-    rh, rl = split(br)
-    ih, il = split(bi)
-    mid = slice(PAD // 2, PAD // 2 + BLK)
-    edge = jnp.zeros((PAD // 2, 2 * WIN), BF)
-    bh = jnp.concatenate([edge, lanes(rh, ih), edge], axis=0)
-    bl = jnp.concatenate([edge, lanes(rl, il), edge], axis=0)
-    o = dot3(rows(rh[mid], ih[mid]), rows(rl[mid], il[mid]), bh, bl)
-    return o[:BLK, :WIN] - o[BLK:, WIN:], o[:BLK, WIN:] + o[BLK:, :WIN]
+def operator_blocks(taps):
+    near, mid = slice(PAD // 2, WIN - PAD // 2), slice(PAD, PAD + BLK)
+
+    def parts(re, im):
+        return [split(re), split(im), split(re + im)]
+
+    def products(three, at):
+        return [dot3(h[at], l[at], h, l) for h, l in three]
+
+    def whole(x):
+        edge = jnp.zeros((PAD // 2, WIN), F32)
+        return jnp.concatenate([edge, x, edge], axis=0)
+
+    ones = [[pltpu.roll(x, 0, 1, stride=1, stride_axis=0) for x in pair] for pair in taps]
+    ones = [parts(*pair) for pair in ones]
+    twos = [products(three, near) for three in ones]
+    twos = [parts(whole(p - q), whole(r - p - q)) for p, q, r in twos]
+    fours = [products(three, mid) for three in twos]
+    return [(p - q, r - p - q) for p, q, r in fours]
 
 
 def upper_half():
@@ -77,20 +78,20 @@
 
 def kernel(
     n_src, n_rcv, n_freq,
-    u_ref, op_ref, vel_ref, idx_ref, wgt_ref, perm_ref,
+    u_any, op_any, vel_any, idx_any, wgt_any, perm_ref,
     out_ref, img_ref,
     raw, turn, mix, crw, cw, w_op, s_op, xh, xl,
     to_l, to_r, from_l, from_r, to_u, to_d, from_u, from_d,
-    img_mine, img_all,
-    r_send, r_recv, s_send, s_recv, f_send, f_recv, known_u, known_d,
+    img_mine, img_all, u_ref, op_ref, vel_ref, idx_ref, wgt_ref,
+    in_sem, r_send, r_recv, s_send, s_recv, f_send, f_recv, known_u, known_d,
 ):
     h = lax.axis_index("src")
     c = lax.axis_index("rcv")
     f = lax.axis_index("freq")
     n_blk = out_ref.shape[2] // BLK
-    n_tile = vel_ref.shape[0]
-    n_tab = op_ref.shape[2]
-    n_vel = idx_ref.shape[1]
+    n_tile = vel_any.shape[0]
+    n_tab = op_any.shape[2]
+    n_vel = idx_any.shape[1]
     has_l, has_r = c > 0, c < n_rcv - 1
     has_u, has_d = h > 0, h < n_src - 1
     owner = h == c // n_blk
@@ -116,6 +117,21 @@
     for d in range(1, n_freq):
         pl.semaphore_signal(barrier, 1, **to("freq", lax.rem(f + d, n_freq)))
 
+    n_row = u_any.shape[2]
+
+    def fetch_lines(part, at, sem):
+        return pltpu.make_async_copy(u_any.at[part, 0, at, :], u_ref.at[part, 0, at, :], in_sem.at[sem])
+
+    outer_lines = [
+        fetch_lines(part, at, 2 * part + k)
+        for part in range(2) for k, at in enumerate([pl.ds(0, PAD), pl.ds(n_row - PAD, PAD)])]
+    inner_lines = [fetch_lines(part, pl.ds(PAD, n_row - 2 * PAD), 4 + part) for part in range(2)]
+    tables = [
+        pltpu.make_async_copy(src, dst, in_sem.at[6 + k])
+        for k, (src, dst) in enumerate([(op_any, op_ref), (idx_any, idx_ref), (wgt_any, wgt_ref), (vel_any, vel_ref)])]
+    for copy in outer_lines + tables + inner_lines:
+        copy.start()
+
     n_mid = n_blk - 1
 
     def chunk_start(p, col):
@@ -150,8 +166,6 @@
     def clear(ref):
         ref[...] = jnp.zeros_like(ref)
 
-    pack(0)
-    pack(1)
     each([
         (jnp.logical_not(has_l), lambda: clear(from_l)),
         (jnp.logical_not(has_r), lambda: clear(from_r)),
@@ -159,6 +173,30 @@
         (jnp.logical_not(has_d), lambda: clear(from_d)),
     ])
 
+    for copy in outer_lines:
+        copy.wait()
+    pack(0)
+    ones = lambda cond: cond.astype(jnp.int32)
+    pl.semaphore_wait(barrier, ones(has_l) + ones(has_r) + ones(has_u) + ones(has_d) + (n_freq - 1))
+
+    def tell(t):
+        each([
+            (has_d if t == 0 else jnp.logical_and(has_d, h >= t), lambda: pl.semaphore_signal(known_u.at[t], 1, **down)),
+            (has_u if t == 0 else jnp.logical_and(has_u, h <= n_src - 1 - t),
+             lambda: pl.semaphore_signal(known_d.at[t], 1, **up)),
+        ])
+
+    def learn(t):
+        each([
+            (h >= t + 1, lambda: pl.semaphore_wait(known_u.at[t], 1)),
+            (h <= n_src - 2 - t, lambda: pl.semaphore_wait(known_d.at[t], 1)),
+        ])
+
+    tell(0)
+    send(0)
+
+    for copy in tables:
+        copy.wait()
     clear(raw)
     clear(turn)
     raw[0, 0:TAPS, :] = op_ref[:, 0, :]
@@ -184,28 +222,6 @@
         part = jnp.where(few, pltpu.roll(turned, (BLK - 32 * p) % BLK, 1), 0.0)
         mix[:, WIN * p:WIN * (p + 1)] = pltpu.roll(lanes(part, none), WIN - TAPS // 2, 1)
 
-    ones = lambda cond: cond.astype(jnp.int32)
-    pl.semaphore_wait(barrier, ones(has_l) + ones(has_r) + ones(has_u) + ones(has_d) + (n_freq - 1))
-    for p in range(HOLD):
-        send(p)
-
-    def tell(t):
-        each([
-            (has_d if t == 0 else jnp.logical_and(has_d, h >= t), lambda: pl.semaphore_signal(known_u.at[t], 1, **down)),
-            (has_u if t == 0 else jnp.logical_and(has_u, h <= n_src - 1 - t),
-             lambda: pl.semaphore_signal(known_d.at[t], 1, **up)),
-        ])
-
-    def learn(t):
-        each([
-            (h >= t + 1, lambda: pl.semaphore_wait(known_u.at[t], 1)),
-            (h <= n_src - 2 - t, lambda: pl.semaphore_wait(known_d.at[t], 1)),
-        ])
-
-    tell(0)
-    for p in range(2, n_blk):
-        pack(p)
-
     def taps_at(dst, first_tile):
         def one(t, _):
             g = first_tile + t
@@ -216,9 +232,30 @@
             return 0
         lax.fori_loop(0, dst.shape[0] // TILE, one, 0)
 
+    for copy in inner_lines:
+        copy.wait()
+    for p in range(1, HOLD):
+        pack(p)
+        send(p)
+    for p in range(HOLD, n_blk):
+        pack(p)
+
     sub = upper_half()
     taps_at(crw, (c * BLK - PAD) // TILE)
-    mr, mi = operator_block(crw[:, :WIN], crw[:, WIN:])
+    taps_at(cw, (h * n_blk * BLK - PAD) // TILE)
+
+    def source_taps(k):
+        r = pl.multiple_of(lax.rem(quarter + k, n_blk) * BLK, BLK)
+        return cw[pl.ds(r, WIN), :WIN], cw[pl.ds(r, WIN), WIN:]
+
+    def keep_source_operator(k, sr, si):
+        b = lax.rem(quarter + k, n_blk)
+        sh, sl = split(rows(sr, si))
+        s_op[b, :, :WIN] = sh
+        s_op[b, :, WIN:] = sl
+
+    (mr, mi), first = operator_blocks([(crw[:, :WIN], crw[:, WIN:]), source_taps(0)])
+    keep_source_operator(0, *first)
     pieces = []
     for m in (mr, mi):
         t = rows(m[:, :BLK].T, m[:, BLK:].T)
@@ -229,15 +266,6 @@
     w_op[0:WIN, :] = wh
     w_op[WIN:2 * WIN, :] = wh
     w_op[2 * WIN:, :] = wl
-    taps_at(cw, (h * n_blk * BLK - PAD) // TILE)
-
-    def make_source_operator(k):
-        b = lax.rem(quarter + k, n_blk)
-        r = pl.multiple_of(b * BLK, BLK)
-        sr, si = operator_block(cw[pl.ds(r, WIN), :WIN], cw[pl.ds(r, WIN), WIN:])
-        sh, sl = split(rows(sr, si))
-        s_op[b, :, :WIN] = sh
-        s_op[b, :, WIN:] = sl
 
     def receivers(p):
         each([(has_r, lambda: copy_l(p).wait_recv()), (has_l, lambda: copy_r(p).wait_recv())])
@@ -262,34 +290,36 @@
             xh[at, :] = xhi
             xl[at, :] = xlo
 
-    make_source_operator(0)
+    if n_src > 2:
+        learn(0)
+        tell(1)
     receivers(0)
     each([(has_u, lambda: copy_u().start()), (has_d, lambda: copy_d().start())])
     for p in range(HOLD, n_blk):
         send(p)
-    for t in range(1, n_src - 1):
+    for k, op in enumerate(operator_blocks([source_taps(k) for k in range(1, n_blk)]), 1):
+        keep_source_operator(k, *op)
+    for t in range(2, n_src - 1):
         learn(t - 1)
         tell(t)
-    make_source_operator(1)
     receivers(1)
-    make_source_operator(2)
-    receivers(2)
-
-    each([(has_u, lambda: copy_d().wait_recv()), (has_d, lambda: copy_u().wait_recv())])
-    zero = jnp.zeros((8, BLK), F32)
-    u8, d8 = from_u[64:72, :], from_d[64:72, :]
-    pad = jnp.zeros((24, 2 * BLK), F32)
-    top = jnp.concatenate([
-        pad,
-        lanes(jnp.where(sub, u8, zero), pltpu.roll(jnp.where(sub, zero, u8), 4, 0)),
-        lanes(from_u[0:32, :], from_u[32:64, :])], axis=0)
-    low = jnp.concatenate([
-        lanes(from_d[0:32, :], from_d[32:64, :]),
-        lanes(jnp.where(sub, zero, d8), pltpu.roll(jnp.where(sub, d8, zero), 4, 0)),
-        pad], axis=0)
-    end = PAD + n_blk * BLK
-    xh[0:PAD, :], xl[0:PAD, :] = split(top)
-    xh[end:end + PAD, :], xl[end:end + PAD, :] = split(low)
+
+    def halo_sources():
+        each([(has_u, lambda: copy_d().wait_recv()), (has_d, lambda: copy_u().wait_recv())])
+        zero = jnp.zeros((8, BLK), F32)
+        u8, d8 = from_u[64:72, :], from_d[64:72, :]
+        pad = jnp.zeros((24, 2 * BLK), F32)
+        top = jnp.concatenate([
+            pad,
+            lanes(jnp.where(sub, u8, zero), pltpu.roll(jnp.where(sub, zero, u8), 4, 0)),
+            lanes(from_u[0:32, :], from_u[32:64, :])], axis=0)
+        low = jnp.concatenate([
+            lanes(from_d[0:32, :], from_d[32:64, :]),
+            lanes(jnp.where(sub, zero, d8), pltpu.roll(jnp.where(sub, d8, zero), 4, 0)),
+            pad], axis=0)
+        end = PAD + n_blk * BLK
+        xh[0:PAD, :], xl[0:PAD, :] = split(top)
+        xh[end:end + PAD, :], xl[end:end + PAD, :] = split(low)
 
     def sources(k):
         b = lax.rem(quarter + k, n_blk)
@@ -303,27 +333,37 @@
     n_peer = n_src * n_freq
 
     def copy_image(d):
-        e = lax.rem(h * n_freq + f + d, n_peer)
+        e = lax.rem(h + lax.rem(n_src // 2 + d // n_freq, n_src), n_src)
         return pltpu.make_async_remote_copy(
             img_mine, img_all.at[f], f_send.at[d], f_recv.at[f],
-            device_id={"src": e // n_freq, "freq": lax.rem(e, n_freq)}, device_id_type=MESH)
-
-    yr = sources(0)
-    learn(n_src - 2)
-
-    @pl.when(owner)
-    def _():
+            device_id={"src": e, "freq": lax.rem(f + d, n_freq)}, device_id_type=MESH)
+
+    own = (n_src - n_src // 2) % n_src * n_freq
+
+    def each_peer(act):
+        def one(d, _):
+            act(copy_image(d))
+            return 0
+        lax.fori_loop(0, own, one, 0)
+        lax.fori_loop(own + 1, n_peer, one, 0)
+
+    def diagonal():
+        yr = sources(0)
+        pl.when(owner)(lambda: hand_out(yr))
+
+    def hand_out(yr):
+        learn(n_src - 2)
         on = lax.broadcasted_iota(jnp.int32, (BLK, BLK), 0) == lax.broadcasted_iota(jnp.int32, (BLK, BLK), 1)
-        diag = jnp.broadcast_to(jnp.sum(jnp.where(on, yr, 0.0), axis=0, keepdims=True), (8, BLK))
+        diag = jnp.sum(jnp.where(on, yr, 0.0), axis=0, keepdims=True)
         img_mine[...] = diag
         img_all[f] = diag
-
-        def start(d, _):
-            copy_image(d).start()
-            return 0
-        lax.fori_loop(1, n_peer, start, 0)
-
-    make_source_operator(3)
+        each_peer(lambda copy: copy.start())
+
+    outer = jnp.logical_or(quarter == 0, quarter == n_blk - 1)
+    inner = jnp.logical_not(outer)
+    each([(outer, halo_sources), (inner, lambda: receivers(2))])
+    diagonal()
+    each([(inner, halo_sources), (outer, lambda: receivers(2))])
     receivers(3)
     for k in range(1, n_blk):
         sources(k)
@@ -335,18 +375,14 @@
                 img_mine, img_all.at[i], f_send.at[0], f_recv.at[i],
                 device_id={"src": h, "freq": f}, device_id_type=MESH).wait_recv()
         return 0
+    pl.when(jnp.logical_not(owner))(lambda: learn(n_src - 2))
     lax.fori_loop(0, n_freq, got, 0)
     total = img_all[0]
     for i in range(1, n_freq):
         total = total + img_all[i]
-    img_ref[...] = total[0:1]
-
-    @pl.when(owner)
-    def _():
-        def sent(d, _):
-            copy_image(d).wait_send()
-            return 0
-        lax.fori_loop(1, n_peer, sent, 0)
+    img_ref[...] = total
+
+    pl.when(owner)(lambda: each_peer(lambda copy: copy.wait_send()))
 
     for p in range(n_blk):
         each([(has_l, lambda: copy_l(p).wait_send()), (has_r, lambda: copy_r(p).wait_send())])
@@ -358,13 +394,14 @@
     n_tab, n_vel = op_table.shape[1], interp_index.shape[0]
     vmem = pl.BlockSpec(memory_space=pltpu.VMEM)
     smem = pl.BlockSpec(memory_space=pltpu.SMEM)
+    stay = pl.BlockSpec(memory_space=pl.ANY)
     dma, flag = pltpu.SemaphoreType.DMA, pltpu.SemaphoreType.REGULAR
     slabs = [pltpu.VMEM((n_blk, SLAB, BLK), F32)] * 4 + [pltpu.VMEM((SLAB, BLK), F32)] * 4
     length = 2 * PAD + n_blk * BLK
     sunk, image = pl.pallas_call(
         functools.partial(kernel, n_src, n_rcv, n_freq),
         out_shape=(pltpu.VMEM(wavefield.shape, F32), pltpu.VMEM((1, BLK), F32)),
-        in_specs=[vmem, vmem, smem, vmem, vmem, smem],
+        in_specs=[stay, stay, stay, stay, stay, smem],
         out_specs=(vmem, vmem),
         scratch_shapes=[
             pltpu.VMEM((2, 32, n_tab), F32),
@@ -377,8 +414,14 @@
             pltpu.VMEM((length, WIN), BF),
             pltpu.VMEM((length, WIN), BF),
             *slabs,
-            pltpu.VMEM((8, BLK), F32),
-            pltpu.VMEM((n_freq, 8, BLK), F32),
+            pltpu.VMEM((1, BLK), F32),
+            pltpu.VMEM((n_freq, 1, BLK), F32),
+            pltpu.VMEM(wavefield.shape, F32),
+            pltpu.VMEM((TAPS, 2, n_tab), F32),
+            pltpu.SMEM(vel_index.shape, jnp.int32),
+            pltpu.VMEM(interp_index.shape[::-1], jnp.int32),
+            pltpu.VMEM(interp_index.shape[::-1], F32),
+            dma((10,)),
             dma((2, n_blk)), dma((2, n_blk)), dma((2,)), dma((2,)),
             dma((n_src * n_freq,)), dma((n_freq,)), flag((n_src - 1,)), flag((n_src - 1,)),
         ],

time: 28.7 us -> 26 us (0.906)
  the two profiles are of different devices: /device:TPU:257 before, /device:TPU:193 now
where the time goes in v3:
time: 26 us; the launch traced here: 25.8 us
  Pallas kernels  23.2 us (89%)
  local copies, waits for them, and re-layouts  1.31 us (5%)
  between operations  1.29 us (5%)
    pallas_call x1, Pallas kernels, body(): pl.pallas_call(functools.partial(kernel, n_src, n_rcv, n_freq), out_shape...  23.2 us
    unnamed x2, local copies, waits for them, and re-layouts  1.31 us

profile of v3, /device:TPU:193, one launch (start us, length us, event | category | flops | bytes accessed | tf_op | source)
XLA Modules:
  0.0 25.8 jit_solution(6185638505224441435)
XLA Ops:
  1.3 23.2 %depth_step.1 = (f32[2,1,512,128]{3,2,1,0:T(8,128)S(1)}, f32[1,128]{1,0:T(1,128)S(1)}) custom-call(f32[2,1,512,128]{3,2,1,0:T(8,128)} %u_any.1, f32[19,2,64]{2,1,0:T(2,128)} %bitcast.5, s32[128]{0:T(128)} %vel_any.1, s32[8,16]{1,0:T(8,128)} %bitcast.6, f32[8,16]{1,0:T(8,128)} %bitcast.7, s32[1]{0:T(128)S(6)} %copy.12.perm_ref), custom_call_target="tpu_custom_call" | custom-call | tf_op jit(solution)/shard_map/depth_step/pallas_call | solution.py:401
  24.5 0.8 %copy.10 = f32[2,1,512,128]{3,2,1,0:T(8,128)} copy(f32[2,1,512,128]{3,2,1,0:T(8,128)S(1)} %get-tuple-element.6) | data formatting | bytes 1048576
  25.3 0.5 %copy.11 = f32[128]{0:T(128)} copy(f32[128]{0:T(128)S(1)} %bitcast.4) | data formatting | bytes 1024

commit v4 on v3

--- a/solution.py
+++ b/solution.py
@@ -16,7 +16,7 @@
 BLK = 128
 PAD = 64
 WIN = 256
-HOLD = 2
+HOLD = 3
 SLAB = 72
 
 
@@ -78,11 +78,11 @@
 
 def kernel(
     n_src, n_rcv, n_freq,
-    u_any, op_any, vel_any, idx_any, wgt_any, perm_ref,
+    u_any, op_any, vel_any, idx_any, wgt_any, perm_any,
     out_ref, img_ref,
-    raw, turn, mix, crw, cw, w_op, s_op, xh, xl,
+    raw, turn, mix, crw, cw, w_op, s_op, xh, xl, gh, gl,
     to_l, to_r, from_l, from_r, to_u, to_d, from_u, from_d,
-    img_mine, img_all, u_ref, op_ref, vel_ref, idx_ref, wgt_ref,
+    img_mine, img_all, u_ref, op_ref, vel_ref, idx_ref, wgt_ref, perm_ref,
     in_sem, r_send, r_recv, s_send, s_recv, f_send, f_recv, known_u, known_d,
 ):
     h = lax.axis_index("src")
@@ -96,6 +96,9 @@
     has_u, has_d = h > 0, h < n_src - 1
     owner = h == c // n_blk
     quarter = lax.rem(c, n_blk)
+    first, final = quarter == 0, quarter == n_blk - 1
+    helped = jnp.logical_or(jnp.logical_and(first, c // n_blk > 0), jnp.logical_and(final, c // n_blk < n_src - 1))
+    helper = jnp.logical_and(helped, h == c // n_blk + jnp.where(first, -1, 1))
 
     def to(axis, index):
         return dict(device_id={axis: index}, device_id_type=MESH)
@@ -128,7 +131,8 @@
     inner_lines = [fetch_lines(part, pl.ds(PAD, n_row - 2 * PAD), 4 + part) for part in range(2)]
     tables = [
         pltpu.make_async_copy(src, dst, in_sem.at[6 + k])
-        for k, (src, dst) in enumerate([(op_any, op_ref), (idx_any, idx_ref), (wgt_any, wgt_ref), (vel_any, vel_ref)])]
+        for k, (src, dst) in enumerate([(op_any, op_ref), (idx_any, idx_ref), (wgt_any, wgt_ref), (vel_any, vel_ref),
+                                     (perm_any, perm_ref)])]
     for copy in outer_lines + tables + inner_lines:
         copy.start()
 
@@ -171,7 +175,12 @@
         (jnp.logical_not(has_r), lambda: clear(from_r)),
         (jnp.logical_not(has_u), lambda: clear(from_u)),
         (jnp.logical_not(has_d), lambda: clear(from_d)),
+        (jnp.logical_not(helped), lambda: clear(img_all.at[pl.ds(n_freq, n_freq)])),
     ])
+    edge = PAD + n_blk * BLK
+    for x in (xh, xl):
+        clear(x.at[pl.ds(0, PAD)])
+        clear(x.at[pl.ds(edge, PAD)])
 
     for copy in outer_lines:
         copy.wait()
@@ -234,10 +243,9 @@
 
     for copy in inner_lines:
         copy.wait()
-    for p in range(1, HOLD):
-        pack(p)
-        send(p)
-    for p in range(HOLD, n_blk):
+    pack(1)
+    send(1)
+    for p in range(2, n_blk):
         pack(p)
 
     sub = upper_half()
@@ -254,8 +262,8 @@
         s_op[b, :, :WIN] = sh
         s_op[b, :, WIN:] = sl
 
-    (mr, mi), first = operator_blocks([(crw[:, :WIN], crw[:, WIN:]), source_taps(0)])
-    keep_source_operator(0, *first)
+    (mr, mi), nearest = operator_blocks([(crw[:, :WIN], crw[:, WIN:]), source_taps(0)])
+    keep_source_operator(0, *nearest)
     pieces = []
     for m in (mr, mi):
         t = rows(m[:, :BLK].T, m[:, BLK:].T)
@@ -293,17 +301,12 @@
     if n_src > 2:
         learn(0)
         tell(1)
+    for p in range(2, HOLD):
+        send(p)
     receivers(0)
     each([(has_u, lambda: copy_u().start()), (has_d, lambda: copy_d().start())])
     for p in range(HOLD, n_blk):
         send(p)
-    for k, op in enumerate(operator_blocks([source_taps(k) for k in range(1, n_blk)]), 1):
-        keep_source_operator(k, *op)
-    for t in range(2, n_src - 1):
-        learn(t - 1)
-        tell(t)
-    receivers(1)
-
     def halo_sources():
         each([(has_u, lambda: copy_d().wait_recv()), (has_d, lambda: copy_u().wait_recv())])
         zero = jnp.zeros((8, BLK), F32)
@@ -321,21 +324,24 @@
         xh[0:PAD, :], xl[0:PAD, :] = split(top)
         xh[end:end + PAD, :], xl[end:end + PAD, :] = split(low)
 
-    def sources(k):
+    def source_block(k):
         b = lax.rem(quarter + k, n_blk)
         r = pl.multiple_of(b * BLK, BLK)
         o = dot3(s_op[b, :, :WIN], s_op[b, :, WIN:], xh[pl.ds(r, WIN), :], xl[pl.ds(r, WIN), :])
-        yr = o[:BLK, :BLK] - o[BLK:, BLK:]
-        out_ref[0, 0, pl.ds(r, BLK), :] = yr
+        return r, o
+
+    def sources(k):
+        r, o = source_block(k)
+        out_ref[0, 0, pl.ds(r, BLK), :] = o[:BLK, :BLK] - o[BLK:, BLK:]
         out_ref[1, 0, pl.ds(r, BLK), :] = o[:BLK, BLK:] + o[BLK:, :BLK]
-        return yr
 
     n_peer = n_src * n_freq
+    mine = f + jnp.where(helper, n_freq, 0)
 
     def copy_image(d):
         e = lax.rem(h + lax.rem(n_src // 2 + d // n_freq, n_src), n_src)
         return pltpu.make_async_remote_copy(
-            img_mine, img_all.at[f], f_send.at[d], f_recv.at[f],
+            img_mine, img_all.at[mine], f_send.at[d], f_recv.at[mine],
             device_id={"src": e, "freq": lax.rem(f + d, n_freq)}, device_id_type=MESH)
 
     own = (n_src - n_src // 2) % n_src * n_freq
@@ -347,53 +353,78 @@
         lax.fori_loop(0, own, one, 0)
         lax.fori_loop(own + 1, n_peer, one, 0)
 
+    def keep_diagonal(o):
+        on = lax.broadcasted_iota(jnp.int32, (BLK, BLK), 0) == lax.broadcasted_iota(jnp.int32, (BLK, BLK), 1)
+        block = o[:BLK, :BLK] - o[BLK:, BLK:]
+        diag = jnp.sum(jnp.where(on, block, 0.0), axis=0, keepdims=True)
+        img_mine[...] = diag
+        img_all[mine] = diag
+
+    def hand_out():
+        learn(n_src - 2)
+        each_peer(lambda copy: copy.start())
+
     def diagonal():
-        yr = sources(0)
-        pl.when(owner)(lambda: hand_out(yr))
-
-    def hand_out(yr):
-        learn(n_src - 2)
-        on = lax.broadcasted_iota(jnp.int32, (BLK, BLK), 0) == lax.broadcasted_iota(jnp.int32, (BLK, BLK), 1)
-        diag = jnp.sum(jnp.where(on, yr, 0.0), axis=0, keepdims=True)
-        img_mine[...] = diag
-        img_all[f] = diag
-        each_peer(lambda copy: copy.start())
-
-    outer = jnp.logical_or(quarter == 0, quarter == n_blk - 1)
-    inner = jnp.logical_not(outer)
-    each([(outer, halo_sources), (inner, lambda: receivers(2))])
-    diagonal()
-    each([(inner, halo_sources), (outer, lambda: receivers(2))])
+        keep_diagonal(source_block(0)[1])
+        hand_out()
+
+    def help_diagonal():
+        b = jnp.where(first, n_blk, -1)
+        taps_at(crw, ((h * n_blk + b) * BLK - PAD) // TILE)
+        sr, si = operator_blocks([(crw[:, :WIN], crw[:, WIN:])])[0]
+        sh, sl = split(rows(sr, si))
+        clear(gh)
+        clear(gl)
+        at = pl.ds(pl.multiple_of(jnp.where(first, 0, WIN - PAD), PAD), PAD)
+        own = pl.ds(pl.multiple_of(jnp.where(first, edge - PAD, PAD), PAD), PAD)
+        gh[at, :] = xh[own, :]
+        gl[at, :] = xl[own, :]
+        keep_diagonal(dot3(sh, sl, gh[...], gl[...]))
+
+    pl.when(helper)(help_diagonal)
+    for t in range(2, n_src - 1):
+        learn(t - 1)
+        tell(t)
+    pl.when(helper)(hand_out)
+    receivers(1)
+    outer = jnp.logical_or(first, final)
+    pl.when(jnp.logical_and(owner, outer))(diagonal)
+    for k, op in enumerate(operator_blocks([source_taps(k) for k in range(1, n_blk)]), 1):
+        keep_source_operator(k, *op)
+    receivers(2)
+    pl.when(jnp.logical_and(owner, jnp.logical_not(outer)))(diagonal)
+    halo_sources()
     receivers(3)
-    for k in range(1, n_blk):
+    for k in range(n_blk):
         sources(k)
 
     def got(i, _):
-        @pl.when(jnp.logical_not(jnp.logical_and(owner, f == i)))
+        sender, there = jnp.where(i < n_freq, owner, helper), jnp.where(i < n_freq, True, helped)
+
+        @pl.when(jnp.logical_and(there, jnp.logical_not(jnp.logical_and(sender, f == lax.rem(i, n_freq)))))
         def _():
             pltpu.make_async_remote_copy(
                 img_mine, img_all.at[i], f_send.at[0], f_recv.at[i],
                 device_id={"src": h, "freq": f}, device_id_type=MESH).wait_recv()
         return 0
-    pl.when(jnp.logical_not(owner))(lambda: learn(n_src - 2))
-    lax.fori_loop(0, n_freq, got, 0)
-    total = img_all[0]
-    for i in range(1, n_freq):
-        total = total + img_all[i]
-    img_ref[...] = total
-
-    pl.when(owner)(lambda: each_peer(lambda copy: copy.wait_send()))
+    giver = jnp.logical_or(owner, helper)
+    pl.when(giver)(lambda: each_peer(lambda copy: copy.wait_send()))
 
     for p in range(n_blk):
         each([(has_l, lambda: copy_l(p).wait_send()), (has_r, lambda: copy_r(p).wait_send())])
     each([(has_u, lambda: copy_u().wait_send()), (has_d, lambda: copy_d().wait_send())])
+    pl.when(jnp.logical_not(giver))(lambda: learn(n_src - 2))
+    lax.fori_loop(0, 2 * n_freq, got, 0)
+    total = img_all[0]
+    for i in range(1, 2 * n_freq):
+        total = total + img_all[i]
+    img_ref[...] = total
 
 
 def body(n_src, n_rcv, n_freq, wavefield, op_table, vel_index, interp_index, interp_weight, freq_perm):
     n_blk = wavefield.shape[2] // BLK
     n_tab, n_vel = op_table.shape[1], interp_index.shape[0]
     vmem = pl.BlockSpec(memory_space=pltpu.VMEM)
-    smem = pl.BlockSpec(memory_space=pltpu.SMEM)
     stay = pl.BlockSpec(memory_space=pl.ANY)
     dma, flag = pltpu.SemaphoreType.DMA, pltpu.SemaphoreType.REGULAR
     slabs = [pltpu.VMEM((n_blk, SLAB, BLK), F32)] * 4 + [pltpu.VMEM((SLAB, BLK), F32)] * 4
@@ -401,7 +432,7 @@
     sunk, image = pl.pallas_call(
         functools.partial(kernel, n_src, n_rcv, n_freq),
         out_shape=(pltpu.VMEM(wavefield.shape, F32), pltpu.VMEM((1, BLK), F32)),
-        in_specs=[stay, stay, stay, stay, stay, smem],
+        in_specs=[stay] * 6,
         out_specs=(vmem, vmem),
         scratch_shapes=[
             pltpu.VMEM((2, 32, n_tab), F32),
@@ -413,17 +444,20 @@
             pltpu.VMEM((n_blk, WIN, 2 * WIN), BF),
             pltpu.VMEM((length, WIN), BF),
             pltpu.VMEM((length, WIN), BF),
+            pltpu.VMEM((WIN, WIN), BF),
+            pltpu.VMEM((WIN, WIN), BF),
             *slabs,
             pltpu.VMEM((1, BLK), F32),
-            pltpu.VMEM((n_freq, 1, BLK), F32),
+            pltpu.VMEM((2 * n_freq, 1, BLK), F32),
             pltpu.VMEM(wavefield.shape, F32),
             pltpu.VMEM((TAPS, 2, n_tab), F32),
             pltpu.SMEM(vel_index.shape, jnp.int32),
             pltpu.VMEM(interp_index.shape[::-1], jnp.int32),
             pltpu.VMEM(interp_index.shape[::-1], F32),
-            dma((10,)),
+            pltpu.SMEM(freq_perm.shape, jnp.int32),
+            dma((11,)),
             dma((2, n_blk)), dma((2, n_blk)), dma((2,)), dma((2,)),
-            dma((n_src * n_freq,)), dma((n_freq,)), flag((n_src - 1,)), flag((n_src - 1,)),
+            dma((n_src * n_freq,)), dma((2 * n_freq,)), flag((n_src - 1,)), flag((n_src - 1,)),
         ],
         compiler_params=pltpu.CompilerParams(collective_id=0, has_side_effects=True),
         name="depth_step",

time: 26 us -> 24.4 us (0.938)
  the two profiles are of different devices: /device:TPU:193 before, /device:TPU:200 now
where the time goes in v4:
time: 24.4 us; the launch traced here: 24.3 us
  Pallas kernels  21.7 us (89%)
  local copies, waits for them, and re-layouts  1.31 us (5%)
  between operations  1.29 us (5%)
    pallas_call x1, Pallas kernels, body(): pl.pallas_call(functools.partial(kernel, n_src, n_rcv, n_freq), out_shape...  21.7 us
    unnamed x2, local copies, waits for them, and re-layouts  1.31 us

profile of v4, /device:TPU:200, one launch (start us, length us, event | category | flops | bytes accessed | tf_op | source)
XLA Modules:
  0.0 24.3 jit_solution(13032755359196658857)
XLA Ops:
  1.3 21.7 %depth_step.1 = (f32[2,1,512,128]{3,2,1,0:T(8,128)S(1)}, f32[1,128]{1,0:T(1,128)S(1)}) custom-call(f32[2,1,512,128]{3,2,1,0:T(8,128)} %u_any.1, f32[19,2,64]{2,1,0:T(2,128)} %bitcast.5, s32[128]{0:T(128)} %vel_any.1, s32[8,16]{1,0:T(8,128)} %bitcast.6, f32[8,16]{1,0:T(8,128)} %bitcast.7, s32[1]{0:T(128)S(6)} %copy.12.perm_any), custom_call_target="tpu_custom_call" | custom-call | tf_op jit(solution)/shard_map/depth_step/pallas_call | solution.py:432
  23.0 0.8 %copy.10 = f32[2,1,512,128]{3,2,1,0:T(8,128)} copy(f32[2,1,512,128]{3,2,1,0:T(8,128)S(1)} %get-tuple-element.6) | data formatting | bytes 1048576
  23.8 0.5 %copy.11 = f32[128]{0:T(128)} copy(f32[128]{0:T(128)S(1)} %bitcast.4) | data formatting | bytes 1024

commit v5 on v4

--- a/solution.py
+++ b/solution.py
@@ -80,9 +80,9 @@
     n_src, n_rcv, n_freq,
     u_any, op_any, vel_any, idx_any, wgt_any, perm_any,
     out_ref, img_ref,
-    raw, turn, mix, crw, cw, w_op, s_op, xh, xl, gh, gl,
+    raw, turn, mix, crw, cw, w_op, s_op, h_op, xh, xl, gh, gl,
     to_l, to_r, from_l, from_r, to_u, to_d, from_u, from_d,
-    img_mine, img_all, u_ref, op_ref, vel_ref, idx_ref, wgt_ref, perm_ref,
+    img_mine, img_all, img_out, u_ref, op_ref, vel_ref, idx_ref, wgt_ref, perm_ref,
     in_sem, r_send, r_recv, s_send, s_recv, f_send, f_recv, known_u, known_d,
 ):
     h = lax.axis_index("src")
@@ -110,6 +110,16 @@
         for cond, act in pairs:
             pl.when(cond)(act)
 
+    n_row = u_any.shape[2]
+
+    def fetch_lines(start, size, sem):
+        at = pl.ds(start, size)
+        return pltpu.make_async_copy(u_any.at[:, 0, at, :], u_ref.at[:, 0, at, :], in_sem.at[sem])
+
+    outer_lines = [fetch_lines(0, PAD, 0), fetch_lines(n_row - PAD, PAD, 1)]
+    for copy in outer_lines:
+        copy.start()
+
     barrier = pltpu.get_barrier_semaphore()
     each([
         (has_l, lambda: pl.semaphore_signal(barrier, 1, **left)),
@@ -120,20 +130,12 @@
     for d in range(1, n_freq):
         pl.semaphore_signal(barrier, 1, **to("freq", lax.rem(f + d, n_freq)))
 
-    n_row = u_any.shape[2]
-
-    def fetch_lines(part, at, sem):
-        return pltpu.make_async_copy(u_any.at[part, 0, at, :], u_ref.at[part, 0, at, :], in_sem.at[sem])
-
-    outer_lines = [
-        fetch_lines(part, at, 2 * part + k)
-        for part in range(2) for k, at in enumerate([pl.ds(0, PAD), pl.ds(n_row - PAD, PAD)])]
-    inner_lines = [fetch_lines(part, pl.ds(PAD, n_row - 2 * PAD), 4 + part) for part in range(2)]
+    inner_lines = [fetch_lines(PAD, n_row - 2 * PAD, 2)]
     tables = [
-        pltpu.make_async_copy(src, dst, in_sem.at[6 + k])
+        pltpu.make_async_copy(src, dst, in_sem.at[3 + k])
         for k, (src, dst) in enumerate([(op_any, op_ref), (idx_any, idx_ref), (wgt_any, wgt_ref), (vel_any, vel_ref),
                                      (perm_any, perm_ref)])]
-    for copy in outer_lines + tables + inner_lines:
+    for copy in tables + inner_lines:
         copy.start()
 
     n_mid = n_blk - 1
@@ -149,14 +151,19 @@
         return u_ref[part, 0, pl.ds(chunk_start(p, col), BLK), :]
 
     def pack(p):
+        if p == 0:
+            tr, ti = part_lines(0, 0, c).T, part_lines(1, 0, c).T
+            pack_first(to_l.at[0], tr, ti)
+            pack_last(to_r.at[0], tr, ti)
+            return
         pack_first(to_l.at[p], part_lines(0, p, jnp.maximum(c - 1, 0)).T, part_lines(1, p, jnp.maximum(c - 1, 0)).T)
         pack_last(to_r.at[p], part_lines(0, p, c + 1).T, part_lines(1, p, c + 1).T)
 
     def copy_l(p):
-        return pltpu.make_async_remote_copy(to_l.at[p], from_r.at[p], r_send.at[0, p], r_recv.at[0, p], **left)
+        return pltpu.make_async_remote_copy(to_l.at[p], from_r.at[p], r_send.at[0], r_recv.at[0, p], **left)
 
     def copy_r(p):
-        return pltpu.make_async_remote_copy(to_r.at[p], from_l.at[p], r_send.at[1, p], r_recv.at[1, p], **right)
+        return pltpu.make_async_remote_copy(to_r.at[p], from_l.at[p], r_send.at[1], r_recv.at[1, p], **right)
 
     def copy_u():
         return pltpu.make_async_remote_copy(to_u, from_d, s_send.at[0], s_recv.at[0], **up)
@@ -175,12 +182,7 @@
         (jnp.logical_not(has_r), lambda: clear(from_r)),
         (jnp.logical_not(has_u), lambda: clear(from_u)),
         (jnp.logical_not(has_d), lambda: clear(from_d)),
-        (jnp.logical_not(helped), lambda: clear(img_all.at[pl.ds(n_freq, n_freq)])),
     ])
-    edge = PAD + n_blk * BLK
-    for x in (xh, xl):
-        clear(x.at[pl.ds(0, PAD)])
-        clear(x.at[pl.ds(edge, PAD)])
 
     for copy in outer_lines:
         copy.wait()
@@ -204,6 +206,11 @@
     tell(0)
     send(0)
 
+    edge = PAD + n_blk * BLK
+    for x in (xh, xl):
+        clear(x.at[pl.ds(0, PAD)])
+        clear(x.at[pl.ds(edge, PAD)])
+    pl.when(jnp.logical_not(helped))(lambda: clear(img_all.at[pl.ds(n_freq, n_freq)]))
     for copy in tables:
         copy.wait()
     clear(raw)
@@ -303,6 +310,16 @@
         tell(1)
     for p in range(2, HOLD):
         send(p)
+
+    def make_helper_operator():
+        b = jnp.where(first, n_blk, -1)
+        taps_at(crw, ((h * n_blk + b) * BLK - PAD) // TILE)
+        sr, si = operator_blocks([(crw[:, :WIN], crw[:, WIN:])])[0]
+        sh, sl = split(rows(sr, si))
+        h_op[:, :WIN] = sh
+        h_op[:, WIN:] = sl
+
+    pl.when(helper)(make_helper_operator)
     receivers(0)
     each([(has_u, lambda: copy_u().start()), (has_d, lambda: copy_d().start())])
     for p in range(HOLD, n_blk):
@@ -335,23 +352,20 @@
         out_ref[0, 0, pl.ds(r, BLK), :] = o[:BLK, :BLK] - o[BLK:, BLK:]
         out_ref[1, 0, pl.ds(r, BLK), :] = o[:BLK, BLK:] + o[BLK:, :BLK]
 
-    n_peer = n_src * n_freq
     mine = f + jnp.where(helper, n_freq, 0)
 
-    def copy_image(d):
-        e = lax.rem(h + lax.rem(n_src // 2 + d // n_freq, n_src), n_src)
-        return pltpu.make_async_remote_copy(
-            img_mine, img_all.at[mine], f_send.at[d], f_recv.at[mine],
-            device_id={"src": e, "freq": lax.rem(f + d, n_freq)}, device_id_type=MESH)
-
-    own = (n_src - n_src // 2) % n_src * n_freq
-
-    def each_peer(act):
+    near = jnp.where(h == n_src - 1, n_src - 1, 1)
+    groups = [n_src // 2, near, 0, n_src - near] if n_src == 4 else [*range(1, n_src), 0]
+
+    def each_peer(group, act):
         def one(d, _):
-            act(copy_image(d))
+            act(pltpu.make_async_remote_copy(
+                img_mine, img_all.at[mine], f_send, f_recv.at[jnp.where(helper, 1, 0)],
+                device_id={"src": lax.rem(h + groups[group], n_src), "freq": lax.rem(f + d, n_freq)},
+                device_id_type=MESH))
             return 0
-        lax.fori_loop(0, own, one, 0)
-        lax.fori_loop(own + 1, n_peer, one, 0)
+        own = isinstance(groups[group], int) and groups[group] == 0
+        lax.fori_loop(int(own), n_freq, one, 0)
 
     def keep_diagonal(o):
         on = lax.broadcasted_iota(jnp.int32, (BLK, BLK), 0) == lax.broadcasted_iota(jnp.int32, (BLK, BLK), 1)
@@ -361,25 +375,25 @@
         img_all[mine] = diag
 
     def hand_out():
+        for group in range(n_src - 1):
+            each_peer(group, lambda copy: copy.start())
+
+    def hand_last():
         learn(n_src - 2)
-        each_peer(lambda copy: copy.start())
+        each_peer(n_src - 1, lambda copy: copy.start())
 
     def diagonal():
         keep_diagonal(source_block(0)[1])
         hand_out()
 
     def help_diagonal():
-        b = jnp.where(first, n_blk, -1)
-        taps_at(crw, ((h * n_blk + b) * BLK - PAD) // TILE)
-        sr, si = operator_blocks([(crw[:, :WIN], crw[:, WIN:])])[0]
-        sh, sl = split(rows(sr, si))
         clear(gh)
         clear(gl)
         at = pl.ds(pl.multiple_of(jnp.where(first, 0, WIN - PAD), PAD), PAD)
         own = pl.ds(pl.multiple_of(jnp.where(first, edge - PAD, PAD), PAD), PAD)
         gh[at, :] = xh[own, :]
         gl[at, :] = xl[own, :]
-        keep_diagonal(dot3(sh, sl, gh[...], gl[...]))
+        keep_diagonal(dot3(h_op[:, :WIN], h_op[:, WIN:], gh[...], gl[...]))
 
     pl.when(helper)(help_diagonal)
     for t in range(2, n_src - 1):
@@ -391,30 +405,48 @@
     pl.when(jnp.logical_and(owner, outer))(diagonal)
     for k, op in enumerate(operator_blocks([source_taps(k) for k in range(1, n_blk)]), 1):
         keep_source_operator(k, *op)
+    giver = jnp.logical_or(owner, helper)
+    inner = jnp.logical_and(owner, jnp.logical_not(outer))
+    pl.when(jnp.logical_and(giver, jnp.logical_not(inner)))(hand_last)
     receivers(2)
-    pl.when(jnp.logical_and(owner, jnp.logical_not(outer)))(diagonal)
+    pl.when(inner)(diagonal)
+    pl.when(inner)(hand_last)
     halo_sources()
     receivers(3)
     for k in range(n_blk):
         sources(k)
 
-    def got(i, _):
-        sender, there = jnp.where(i < n_freq, owner, helper), jnp.where(i < n_freq, True, helped)
-
-        @pl.when(jnp.logical_and(there, jnp.logical_not(jnp.logical_and(sender, f == lax.rem(i, n_freq)))))
-        def _():
-            pltpu.make_async_remote_copy(
-                img_mine, img_all.at[i], f_send.at[0], f_recv.at[i],
-                device_id={"src": h, "freq": f}, device_id_type=MESH).wait_recv()
-        return 0
-    giver = jnp.logical_or(owner, helper)
-    pl.when(giver)(lambda: each_peer(lambda copy: copy.wait_send()))
-
-    for p in range(n_blk):
-        each([(has_l, lambda: copy_l(p).wait_send()), (has_r, lambda: copy_r(p).wait_send())])
-    each([(has_u, lambda: copy_u().wait_send()), (has_d, lambda: copy_d().wait_send())])
-    pl.when(jnp.logical_not(giver))(lambda: learn(n_src - 2))
-    lax.fori_loop(0, 2 * n_freq, got, 0)
+    def line_copy(size, sem):
+        at = pl.ds(0, size)
+        return pltpu.make_async_remote_copy(
+            img_out.at[at], img_out.at[at], f_send, f_recv.at[sem],
+            device_id={"src": h, "freq": f}, device_id_type=MESH)
+
+    all_l = pltpu.make_async_remote_copy(to_l, from_r, r_send.at[0], r_recv.at[0, 0], **left)
+    all_r = pltpu.make_async_remote_copy(to_r, from_l, r_send.at[1], r_recv.at[1, 0], **right)
+    each([
+        (giver, lambda: line_copy(n_src * n_freq - 1, 0).wait_send()),
+        (has_l, all_l.wait_send),
+        (has_r, all_r.wait_send),
+        (has_u, lambda: copy_u().wait_send()),
+        (has_d, lambda: copy_d().wait_send()),
+        (jnp.logical_not(giver), lambda: learn(n_src - 2)),
+    ])
+    not_mine = n_freq - 1
+
+    def got():
+        others, helpers = jnp.logical_not(owner), jnp.logical_and(helped, jnp.logical_not(helper))
+        each([
+            (others, lambda: line_copy(n_freq, 0).wait_recv()),
+            (helpers, lambda: line_copy(n_freq, 1).wait_recv()),
+        ])
+        if not_mine:
+            each([
+                (owner, lambda: line_copy(not_mine, 0).wait_recv()),
+                (helper, lambda: line_copy(not_mine, 1).wait_recv()),
+            ])
+
+    got()
     total = img_all[0]
     for i in range(1, 2 * n_freq):
         total = total + img_all[i]
@@ -442,6 +474,7 @@
             pltpu.VMEM((length, 2 * WIN), F32),
             pltpu.VMEM((3 * WIN, WIN), BF),
             pltpu.VMEM((n_blk, WIN, 2 * WIN), BF),
+            pltpu.VMEM((WIN, 2 * WIN), BF),
             pltpu.VMEM((length, WIN), BF),
             pltpu.VMEM((length, WIN), BF),
             pltpu.VMEM((WIN, WIN), BF),
@@ -449,15 +482,16 @@
             *slabs,
             pltpu.VMEM((1, BLK), F32),
             pltpu.VMEM((2 * n_freq, 1, BLK), F32),
+            pltpu.VMEM((n_src * n_freq, 1, BLK), F32),
             pltpu.VMEM(wavefield.shape, F32),
             pltpu.VMEM((TAPS, 2, n_tab), F32),
             pltpu.SMEM(vel_index.shape, jnp.int32),
             pltpu.VMEM(interp_index.shape[::-1], jnp.int32),
             pltpu.VMEM(interp_index.shape[::-1], F32),
             pltpu.SMEM(freq_perm.shape, jnp.int32),
-            dma((11,)),
-            dma((2, n_blk)), dma((2, n_blk)), dma((2,)), dma((2,)),
-            dma((n_src * n_freq,)), dma((2 * n_freq,)), flag((n_src - 1,)), flag((n_src - 1,)),
+            dma((8,)),
+            dma((2,)), dma((2, n_blk)), dma((2,)), dma((2,)),
+            dma, dma((2,)), flag((n_src - 1,)), flag((n_src - 1,)),
         ],
         compiler_params=pltpu.CompilerParams(collective_id=0, has_side_effects=True),
         name="depth_step",

time: 24.4 us -> 24.1 us (0.988)
  Pallas kernels: 21.7 us -> 21.4 us
    pallas_call x1, Pallas kernels: 21.7 us -> 21.4 us  [body(): pl.pallas_call(functools.partial(kernel, n_src, n_rcv, n_freq), out_shape...]
where the time goes in v5:
time: 24.1 us; the launch traced here: 24 us
  Pallas kernels  21.4 us (89%)
  local copies, waits for them, and re-layouts  1.31 us (5%)
  between operations  1.29 us (5%)
    pallas_call x1, Pallas kernels, body(): pl.pallas_call(functools.partial(kernel, n_src, n_rcv, n_freq), out_shape...  21.4 us
    unnamed x2, local copies, waits for them, and re-layouts  1.31 us

profile of v5, /device:TPU:200, one launch (start us, length us, event | category | flops | bytes accessed | tf_op | source)
XLA Modules:
  0.0 24.0 jit_solution(7480821570735316962)
XLA Ops:
  1.3 21.4 %depth_step.1 = (f32[2,1,512,128]{3,2,1,0:T(8,128)S(1)}, f32[1,128]{1,0:T(1,128)S(1)}) custom-call(f32[2,1,512,128]{3,2,1,0:T(8,128)} %u_any.1, f32[19,2,64]{2,1,0:T(2,128)} %bitcast.5, s32[128]{0:T(128)} %vel_any.1, s32[8,16]{1,0:T(8,128)} %bitcast.6, f32[8,16]{1,0:T(8,128)} %bitcast.7, s32[1]{0:T(128)S(6)} %copy.12.perm_any), custom_call_target="tpu_custom_call" | custom-call | tf_op jit(solution)/shard_map/depth_step/pallas_call | solution.py:464
  22.7 0.8 %copy.10 = f32[2,1,512,128]{3,2,1,0:T(8,128)} copy(f32[2,1,512,128]{3,2,1,0:T(8,128)S(1)} %get-tuple-element.6) | data formatting | bytes 1048576
  23.5 0.5 %copy.11 = f32[128]{0:T(128)} copy(f32[128]{0:T(128)S(1)} %bitcast.4) | data formatting | bytes 1024
